TPU v7x, 512 devices: a whole 4x4x16 slice. The times are simulated.
512 devices in a mesh: blk: 32 (over z_lo, y), seq: 16 (over z_hi, x, core).
Axes of the slice: x: 4, y: 4, z: 16 (z_hi: 2, z_lo: 8; z = z_hi * 8 + z_lo), core: 2. Of those that a mesh axis runs over, the one named last changes fastest.
Arguments:
- tokens: bfloat16 [12288, 4096], P('seq', 'blk'), may hold values from -6 to 6
- grad_out: bfloat16 [12288, 4096], P('seq', 'blk'), may hold values from -0.0546875 to 0.0546875
- input_weight_blocks: bfloat16 [1024, 128, 128], P('blk'), may hold values from -0.25 to 0.25
- output_weight_blocks: bfloat16 [1024, 128, 128], P('blk'), may hold values from -0.25 to 0.25
- row_ids: int32 [1024], P('blk'), may hold values from 0 to 31, as said below
- lengths: int32 [16], P('seq'), may hold values from 1 to 768, 7680 in all
Outputs:
- grad_in: bfloat16 [1024, 128, 128], P('blk', 'seq')
- grad_w_out: bfloat16 [1024, 128, 128], P('blk', 'seq')
Inputs may be any that keep to these rules, and one draw needn't show every extreme that they name: `row_ids`: the 4 blocks of each hidden column block have distinct row blocks. `lengths`: some window is full.
All inputs are finite; a program needn't handle non-finite values. No bound on the sum of `lengths` on one device may be relied on, other than what follows from the above.
Results may differ from a plain program's by a relative error of at most 0.015.
Values may be sent and summed in bfloat16 or wider, within the bound.
No kernel may reach another device: no remote copies, remote signals or barrier semaphores. Data moves between devices by JAX's collectives and lax.ppermute only.
A program may use at most 64 MiB of HBM per device.

v0:
```python
import functools

import jax
import jax.numpy as jnp
from jax import lax
from jax.experimental import pallas as pl
from jax.experimental.pallas import tpu as pltpu
from jax.sharding import PartitionSpec as P

SIDE = 128
PER_COLUMN = 4
N_SEQ = 16
N_X = 4
N_Y = 4
N_Z = 8
N_DEAL = 8
LIVE = 7680
SIZES = (512, 576, 640, 768)
NOTE_ROWS = 8
CHUNKS = 4
DEAD = 256.0
RING = (0, 2, 4, 6, 7, 5, 3, 1)
PLACE = tuple(RING.index(z) for z in range(N_Z))
AXES = ("blk", "seq")
BATCHES = (((0, 1), 1), ((2, 7), 3), ((3, 4), 1), ((5, 6), 3))

gelu_scale = 0.7978845608


def gelu_pair(pre_act):
    tanh_val = jnp.tanh(gelu_scale * (pre_act + 0.044715 * pre_act * pre_act * pre_act))
    activation = 0.5 * pre_act * (1.0 + tanh_val)
    gelu_slope = 0.5 * (1.0 + tanh_val) + 0.5 * pre_act * (
        1.0 - tanh_val * tanh_val
    ) * gelu_scale * (1.0 + 0.134145 * pre_act * pre_act)
    return (activation, gelu_slope)


def move_z(value, step):
    pairs = [
        (z * N_Y + y, RING[(PLACE[z] + step) % N_Z] * N_Y + y)
        for z in range(N_Z)
        for y in range(N_Y)
    ]
    return lax.ppermute(value, "blk", pairs)


def swap_y(value, mask):
    pairs = [(z * N_Y + y, z * N_Y + (y ^ mask)) for z in range(N_Z) for y in range(N_Y)]
    return lax.ppermute(value, "blk", pairs)


def deal_kernel(length_ref, tokens_ref, grad_ref, out_ref):
    rows = tokens_ref.shape[0]
    out_rows = out_ref.shape[0]
    share, stride = rows // N_DEAL, out_rows // N_DEAL
    at = lax.broadcasted_iota(jnp.int32, (rows, SIDE), 0)
    marked = jnp.where(at < length_ref[0], tokens_ref[...].astype(jnp.float32), DEAD)
    both = jnp.concatenate([marked.astype(jnp.bfloat16), grad_ref[...]], axis=1)
    to = lax.broadcasted_iota(jnp.int32, (out_rows, rows), 0)
    source = lax.broadcasted_iota(jnp.int32, (out_rows, rows), 1)
    slot = source % N_DEAL * stride + source // N_DEAL
    pick = jnp.where(slot == to, 1.0, 0.0).astype(jnp.bfloat16)
    dealt = jnp.dot(pick, both, preferred_element_type=jnp.float32)
    place = place_in_share(out_rows, 2 * SIDE, stride)
    high = DEAD + 2.0 * (length_ref[0] // 32).astype(jnp.float32)
    low = DEAD + 2.0 * (length_ref[0] % 32).astype(jnp.float32)
    note = jnp.where(place == share, high, jnp.where(place == share + 1, low, DEAD))
    out_ref[...] = jnp.where(place < share, dealt, note).astype(jnp.bfloat16)


def place_in_share(rows, lanes, stride):
    row = lax.broadcasted_iota(jnp.int32, (rows, lanes), 0)
    start = jnp.zeros_like(row)
    for j in range(1, rows // stride):
        start = jnp.where(row >= j * stride, j * stride, start)
    return row - start


def pack_kernel(dealt_ref, out_ref, size_ref):
    rows, out_rows = dealt_ref.shape[0], out_ref.shape[0]
    share = out_rows // N_DEAL
    values = dealt_ref[:, :SIDE].astype(jnp.float32)
    live = jnp.broadcast_to(jnp.where(values[:, :1] < DEAD / 2, 1.0, 0.0), (rows, SIDE))
    place = place_in_share(rows, SIDE, rows // N_DEAL)
    weight = jnp.where(place == share, 16.0, jnp.where(place == share + 1, 0.5, 0.0))
    lane = lax.broadcasted_iota(jnp.int32, (rows, SIDE), 1)
    held = jnp.sum(jnp.where(lane == 0, weight * (values - DEAD), 0.0))
    most = jnp.maximum(held, LIVE - held).astype(jnp.int32) + (N_DEAL - 1) * N_DEAL
    size = jnp.int32(0)
    for smaller in SIZES[:-1]:
        size = size + (most > smaller * N_DEAL).astype(jnp.int32)
    size_ref[0] = size
    to = lax.broadcasted_iota(jnp.int32, (rows, rows), 0)
    source = lax.broadcasted_iota(jnp.int32, (rows, rows), 1)
    before = jnp.where(source < to, 1.0, 0.0).astype(jnp.bfloat16)
    rank = jnp.dot(before, live.astype(jnp.bfloat16), preferred_element_type=jnp.float32)
    rank = jnp.where(live > 0.5, rank, -1.0)[:, :1]
    slot = lax.broadcasted_iota(jnp.int32, (rows, out_rows), 1).astype(jnp.float32)
    pick = jnp.where(rank == slot, 1.0, 0.0).astype(jnp.bfloat16)
    out_ref[...] = lax.dot_general(
        pick, dealt_ref[...], (((0,), (0,)), ((), ())), preferred_element_type=jnp.float32
    ).astype(jnp.bfloat16)


def grad_kernel(slot_ref, core_ref, *refs):
    rows_at_once = refs[0].shape[0] // CHUNKS
    own = refs[:N_Z]
    passed = refs[N_Z : N_Z + 2 * len(BATCHES)]
    w_in_ref, w_out_ref, out_ref, held, hidden, summed, sems = refs[N_Z + 2 * len(BATCHES) :]
    copies = []

    def put(source, target):
        copies.append(pltpu.make_async_copy(source, target, sems.at[len(copies)]))

    for slot in range(N_Z):
        put(own[slot], held.at[slot * N_Y])
    for index, (batch, mask) in enumerate(BATCHES):
        near, far = passed[2 * index : 2 * index + 2]
        for i, slot in enumerate(batch):
            put(near.at[i], held.at[slot * N_Y + mask])
            put(far.at[i], held.at[slot * N_Y + (mask ^ 2)])
            put(far.at[i + len(batch)], held.at[slot * N_Y + 2])
    for copy in copies:
        copy.start()
    for copy in copies:
        copy.wait()
    core = core_ref[0]

    @pl.loop(0, w_in_ref.shape[0] // PER_COLUMN)
    def _(group):
        first = group * PER_COLUMN
        slots = [slot_ref[first + r] for r in range(PER_COLUMN)]
        w_in = jnp.concatenate([w_in_ref[first + r] for r in range(PER_COLUMN)], axis=0)
        w_out = jnp.concatenate([w_out_ref[first + r] for r in range(PER_COLUMN)], axis=1)

        @pl.loop(0, CHUNKS)
        def _(chunk):
            at = pl.ds(pl.multiple_of(chunk * rows_at_once, 16), rows_at_once)
            x = jnp.concatenate([held[s, at, :SIDE] for s in slots], axis=1)
            g = jnp.concatenate([held[s, at, SIDE:] for s in slots], axis=1)
            pre_act = jnp.dot(x, w_in, preferred_element_type=jnp.float32)
            activation, gelu_slope = gelu_pair(pre_act)
            grad_act = lax.dot_general(
                g, w_out, (((1,), (1,)), ((), ())), preferred_element_type=jnp.float32
            )
            hidden[0, at] = (grad_act * gelu_slope).astype(jnp.bfloat16)
            hidden[1, at] = activation.astype(jnp.bfloat16)

        x = jnp.concatenate([held[s, :, :SIDE] for s in slots], axis=1)
        g = jnp.concatenate([held[s, :, SIDE:] for s in slots], axis=1)
        over_rows = (((0,), (0,)), ((), ()))
        shares = (
            lax.dot_general(hidden[0], x, over_rows, preferred_element_type=jnp.float32),
            lax.dot_general(hidden[1], g, over_rows, preferred_element_type=jnp.float32),
        )
        for which, share in enumerate(shares):
            for r in range(PER_COLUMN):
                summed[which, r] = share[:, r * SIDE : (r + 1) * SIDE]

        @pl.loop(0, PER_COLUMN)
        def _(r):
            for which in range(2):
                block = summed[which, r]
                block = (block.T if which == 0 else block).astype(jnp.bfloat16)
                for seq in range(N_SEQ):
                    z_at, x_at, piece = seq // 8, seq % 8 // 2, seq % 2
                    out_ref[jnp.bitwise_xor(core, piece), x_at, z_at, which, first + r] = block[
                        seq * 8 : seq * 8 + 8
                    ]


def gather_and_differentiate(size, packed, slots, core, w_in, w_out):
    vmem = pl.BlockSpec(memory_space=pltpu.VMEM)
    smem = pl.BlockSpec(memory_space=pltpu.SMEM)
    any_space = pl.BlockSpec(memory_space=pl.ANY)
    n_slots = w_in.shape[0]
    blocks = {0: packed[:size]}
    for i in range(1, 5):
        blocks[i] = move_z(blocks[i - 1], 1)
        if i < 4:
            blocks[N_Z - i] = move_z(blocks[(N_Z - i + 1) % N_Z], -1)
    passed = []
    for batch, mask in BATCHES:
        value = jnp.stack([blocks[slot] for slot in batch])
        near = swap_y(value, mask)
        far = swap_y(jnp.concatenate([value, near]), mask ^ 2)
        passed += [near, far]
    return pl.pallas_call(
        grad_kernel,
        out_shape=jax.ShapeDtypeStruct((2, N_X, 2, 2, n_slots, 8, SIDE), jnp.bfloat16),
        in_specs=[smem, smem] + [any_space] * (N_Z + len(passed)) + [vmem, vmem],
        out_specs=vmem,
        scratch_shapes=[
            pltpu.VMEM((N_Y * N_Z, size, 2 * SIDE), jnp.bfloat16),
            pltpu.VMEM((2, size, SIDE), jnp.bfloat16),
            pltpu.VMEM((2, PER_COLUMN, SIDE, SIDE), jnp.float32),
            pltpu.SemaphoreType.DMA((N_Y * N_Z,)),
        ],
        name="weight_grads",
    )(slots, core, *[blocks[i] for i in range(N_Z)], *passed, w_in, w_out)


def shards(tokens, grad_out, input_weight_blocks, output_weight_blocks, row_ids, lengths):
    blk, seq = lax.axis_index("blk"), lax.axis_index("seq")
    rows = tokens.shape[0]
    vmem = pl.BlockSpec(memory_space=pltpu.VMEM)
    smem = pl.BlockSpec(memory_space=pltpu.SMEM)
    dealt = pl.pallas_call(
        deal_kernel,
        out_shape=jax.ShapeDtypeStruct((rows + N_DEAL * NOTE_ROWS, 2 * SIDE), jnp.bfloat16),
        in_specs=[smem, vmem, vmem],
        out_specs=vmem,
        name="deal",
    )(lengths, tokens, grad_out)
    halves = [[h * N_DEAL + i for i in range(N_DEAL)] for h in range(2)]
    dealt = lax.all_to_all(dealt, "seq", 0, 0, axis_index_groups=halves, tiled=True)
    packed, size = pl.pallas_call(
        pack_kernel,
        out_shape=(
            jax.ShapeDtypeStruct((rows, 2 * SIDE), jnp.bfloat16),
            jax.ShapeDtypeStruct((1,), jnp.int32),
        ),
        in_specs=[vmem],
        out_specs=(vmem, smem),
        name="pack",
    )(dealt)

    place = jnp.array(PLACE, jnp.int32)
    z_slot = (place[blk // N_Y] - place[row_ids // N_Y]) % N_Z
    slots = (z_slot * N_Y + jnp.bitwise_xor(blk, row_ids) % N_Y).astype(jnp.int32)
    shares = lax.switch(
        size[0],
        [functools.partial(gather_and_differentiate, n) for n in SIZES],
        packed,
        slots,
        (seq % 2).reshape(1),
        input_weight_blocks,
        output_weight_blocks,
    )

    swap = [(i, i ^ 1) for i in range(N_SEQ)]
    other = lax.ppermute(shares[1], "seq", swap)
    total = (shares[0].astype(jnp.float32) + other.astype(jnp.float32)).astype(jnp.bfloat16)
    along_x = [[h * 8 + x * 2 + c for x in range(N_X)] for h in range(2) for c in range(2)]
    total = lax.all_to_all(total, "seq", 0, 0, axis_index_groups=along_x, tiled=True)
    total = total.astype(jnp.float32).sum(0)
    mine = lax.dynamic_index_in_dim(total, seq // 8, 0, keepdims=False)
    theirs = lax.dynamic_index_in_dim(total, 1 - seq // 8, 0, keepdims=False)
    across = [(i, i ^ 8) for i in range(N_SEQ)]
    theirs = lax.ppermute(theirs.astype(jnp.bfloat16), "seq", across)
    total = (mine + theirs.astype(jnp.float32)).astype(jnp.bfloat16)
    return total[0], total[1]


def solution(mesh):
    return jax.shard_map(
        shards,
        mesh=mesh,
        in_specs=(
            P("seq", "blk"),
            P("seq", "blk"),
            P("blk", None, None),
            P("blk", None, None),
            P("blk"),
            P("seq"),
        ),
        out_specs=(P("blk", "seq", None), P("blk", "seq", None)),
        check_vma=False,
    )
```

profile of v0, /device:TPU:128, one launch (start us, length us, event | category | flops | bytes accessed | tf_op | source)
XLA Modules:
  0.0 229.6 jit_solution(14643723034356889271)
XLA Ops:
  0.6 0.0 copy-start
  0.6 0.0 copy-start.57
  1.3 2.4 %deal.1 = bf16[832,256]{1,0:T(8,128)(2,1)} custom-call(s32[1]{0:T(128)S(6)} %copy.21.length_ref, bf16[768,128]{1,0:T(8,128)(2,1)} %tokens_ref.1, bf16[768,128]{1,0:T(8,128)(2,1)} %grad_ref.1), custom_call_target="tpu_custom_call" | custom-call | tf_op jit(solution)/shard_map/deal/pallas_call | solution.py:209
  3.8 4.3 %all-to-all-start = ((bf16[8,104,256]{2,1,0:T(8,128)(2,1)}), bf16[8,104,256]{2,1,0:T(8,128)(2,1)S(1)}, u32[]{:S(2)}, u32[]{:S(2)}) async-start(bf16[8,104,256]{2,1,0:T(8,128)(2,1)} %bitcast.119), calls=%async_computation | async-start | bytes 851968 | tf_op jit(solution)/shard_map/all_to_all | solution.py:217
  8.1 0.0 copy-done.57
  8.1 0.6 dynamic_slice.10
  8.7 0.7 gather_fusion
  9.4 0.7 fusion.15
  10.1 0.7 xor_compare_fusion
  10.7 6.6 %all-to-all-done = bf16[8,104,256]{2,1,0:T(8,128)(2,1)S(1)} async-done(((bf16[8,104,256]{2,1,0:T(8,128)(2,1)}), bf16[8,104,256]{2,1,0:T(8,128)(2,1)S(1)}, u32[]{:S(2)}, u32[]{:S(2)}) %all-to-all-start) | async-done | bytes 426016 | tf_op jit(solution)/shard_map/all_to_all | solution.py:217
  17.4 0.8 copy-done.48
  18.1 3.2 %pack.1 = (bf16[768,256]{1,0:T(8,128)(2,1)S(1)}, s32[1]{0:T(128)}) custom-call(bf16[832,256]{1,0:T(8,128)(2,1)} %bitcast.118), custom_call_target="tpu_custom_call" | custom-call | tf_op jit(solution)/shard_map/pack/pallas_call | solution.py:218
  22.0 0.6 add.44
  22.5 158.1 %conditional.1 = (bf16[2,4,2,2,32,8,128]{6,5,4,3,2,1,0:T(8,128)(2,1)}) conditional(s32[]{:T(128)} %bitcast.38, (bf16[768,256]{1,0:T(8,128)(2,1)S(1)}, pred[32]{0:T(512)(128)(4,1)S(1)}, pred[]{:T(512)}, bf16[32,128,128]{2,1,0:T(8,128)(2,1)S(1)}, bf16[32,128,128]{2,1,0:T(8,128)(2,1)S(1)}, ...), branch_computations={%region_0.1_spmd, %region_1.2_spmd, %region_2.3_spmd, %region_3.4_... | conditional | flops 7864839 | bytes 91228472 | solution.py:232
  22.6 5.2 %collective-permute-start.15 = (bf16[576,256]{1,0:T(8,128)(2,1)S(1)}, bf16[576,256]{1,0:T(8,128)(2,1)S(1)}, u32[]{:S(2)}, u32[]{:S(2)}) collective-permute-start(bf16[576,256]{1,0:T(8,128)(2,1)S(1)} %get-tuple-element.298.refs_0_), channel_id=1, source_target_pairs={{0,128},{16,144},{32,160},{48,176},{64,0},{80,16},{96,32},{112,48}... | collective-permute-start | bytes 884744 | tf_op jit(solution)/shard_map/cond/branch_1_fun/ppermute | solution.py:45
  27.8 2.8 %collective-permute-start.19 = (bf16[576,256]{1,0:T(8,128)(2,1)S(1)}, bf16[576,256]{1,0:T(8,128)(2,1)S(1)}, u32[]{:S(2)}, u32[]{:S(2)}) collective-permute-start(bf16[576,256]{1,0:T(8,128)(2,1)S(1)} %get-tuple-element.298.refs_0_), channel_id=1, source_target_pairs={{0,64},{16,80},{32,96},{48,112},{64,192},{80,208},{96,224},{112,24... | collective-permute-start | bytes 884744 | tf_op jit(solution)/shard_map/cond/branch_1_fun/ppermute | solution.py:45
  30.6 11.5 %collective-permute-done.15.refs_1_ = bf16[576,256]{1,0:T(8,128)(2,1)S(1)} collective-permute-done((bf16[576,256]{1,0:T(8,128)(2,1)S(1)}, bf16[576,256]{1,0:T(8,128)(2,1)S(1)}, u32[]{:S(2)}, u32[]{:S(2)}) %collective-permute-start.15) | collective-permute-done | bytes 294944 | tf_op jit(solution)/shard_map/cond/branch_1_fun/ppermute | solution.py:45
  42.0 3.5 %collective-permute-start.16 = (bf16[576,256]{1,0:T(8,128)(2,1)S(1)}, bf16[576,256]{1,0:T(8,128)(2,1)S(1)}, u32[]{:S(2)}, u32[]{:S(2)}) collective-permute-start(bf16[576,256]{1,0:T(8,128)(2,1)S(1)} %collective-permute-done.15.refs_1_), channel_id=1, source_target_pairs={{0,128},{16,144},{32,160},{48,176},{64,0},{80,16},{96,32},{112,48}... | collective-permute-start | bytes 884744 | tf_op jit(solution)/shard_map/cond/branch_1_fun/ppermute | solution.py:45
  45.6 0.0 collective-permute-done.19.refs_7_
  45.6 4.4 %collective-permute-start.20 = (bf16[576,256]{1,0:T(8,128)(2,1)S(1)}, bf16[576,256]{1,0:T(8,128)(2,1)S(1)}, u32[]{:S(2)}, u32[]{:S(2)}) collective-permute-start(bf16[576,256]{1,0:T(8,128)(2,1)S(1)} %collective-permute-done.19.refs_7_), channel_id=1, source_target_pairs={{0,64},{16,80},{32,96},{48,112},{64,192},{80,208},{96,224},{112,24... | collective-permute-start | bytes 884744 | tf_op jit(solution)/shard_map/cond/branch_1_fun/ppermute | solution.py:45
  50.0 9.9 %collective-permute-done.16.refs_2_ = bf16[576,256]{1,0:T(8,128)(2,1)S(1)} collective-permute-done((bf16[576,256]{1,0:T(8,128)(2,1)S(1)}, bf16[576,256]{1,0:T(8,128)(2,1)S(1)}, u32[]{:S(2)}, u32[]{:S(2)}) %collective-permute-start.16) | collective-permute-done | bytes 294944 | tf_op jit(solution)/shard_map/cond/branch_1_fun/ppermute | solution.py:45
  59.9 3.9 %collective-permute-start.17 = (bf16[576,256]{1,0:T(8,128)(2,1)S(1)}, bf16[576,256]{1,0:T(8,128)(2,1)S(1)}, u32[]{:S(2)}, u32[]{:S(2)}) collective-permute-start(bf16[576,256]{1,0:T(8,128)(2,1)S(1)} %collective-permute-done.16.refs_2_), channel_id=1, source_target_pairs={{0,128},{16,144},{32,160},{48,176},{64,0},{80,16},{96,32},{112,48}... | collective-permute-start | bytes 884744 | tf_op jit(solution)/shard_map/cond/branch_1_fun/ppermute | solution.py:45
  63.8 0.0 collective-permute-done.20.refs_6_
  63.8 4.0 %collective-permute-start.21 = (bf16[576,256]{1,0:T(8,128)(2,1)S(1)}, bf16[576,256]{1,0:T(8,128)(2,1)S(1)}, u32[]{:S(2)}, u32[]{:S(2)}) collective-permute-start(bf16[576,256]{1,0:T(8,128)(2,1)S(1)} %collective-permute-done.20.refs_6_), channel_id=1, source_target_pairs={{0,64},{16,80},{32,96},{48,112},{64,192},{80,208},{96,224},{112,24... | collective-permute-start | bytes 884744 | tf_op jit(solution)/shard_map/cond/branch_1_fun/ppermute | solution.py:45
  67.9 0.1 pad_maximum_fusion.12
  67.9 3.1 %collective-permute-start.22 = (bf16[2,576,256]{2,1,0:T(8,128)(2,1)S(1)}, bf16[2,576,256]{2,1,0:T(8,128)(2,1)S(1)}, u32[]{:S(2)}, u32[]{:S(2)}) collective-permute-start(bf16[2,576,256]{2,1,0:T(8,128)(2,1)S(1)} %pad_maximum_fusion.12), channel_id=1, source_target_pairs={{0,16},{16,0},{32,48},{48,32},{64,80},{80,64},{96,112},{112,96},{1... | collective-permute-start | bytes 1769480 | tf_op jit(solution)/shard_map/cond/branch_1_fun/ppermute | solution.py:50
  71.0 4.2 %collective-permute-done.17.refs_3_ = bf16[576,256]{1,0:T(8,128)(2,1)S(1)} collective-permute-done((bf16[576,256]{1,0:T(8,128)(2,1)S(1)}, bf16[576,256]{1,0:T(8,128)(2,1)S(1)}, u32[]{:S(2)}, u32[]{:S(2)}) %collective-permute-start.17) | collective-permute-done | bytes 294944 | tf_op jit(solution)/shard_map/cond/branch_1_fun/ppermute | solution.py:45
  75.3 1.9 collective-permute-start.18
  77.2 0.1 pad_maximum_fusion.13
  77.2 6.5 %collective-permute-start.24 = (bf16[2,576,256]{2,1,0:T(8,128)(2,1)S(1)}, bf16[2,576,256]{2,1,0:T(8,128)(2,1)S(1)}, u32[]{:S(2)}, u32[]{:S(2)}) collective-permute-start(bf16[2,576,256]{2,1,0:T(8,128)(2,1)S(1)} %pad_maximum_fusion.13), channel_id=1, source_target_pairs={{0,48},{16,32},{32,16},{48,0},{64,112},{80,96},{96,80},{112,64},{1... | collective-permute-start | bytes 1769480 | tf_op jit(solution)/shard_map/cond/branch_1_fun/ppermute | solution.py:50
  83.7 0.0 collective-permute-done.21.refs_5_
  83.8 0.1 pad_maximum_fusion.15
  83.8 1.9 collective-permute-start.28
  85.8 0.2 collective-permute-done.18.refs_4_
  86.0 0.1 pad_maximum_fusion.14
  86.0 3.9 %collective-permute-start.26 = (bf16[2,576,256]{2,1,0:T(8,128)(2,1)S(1)}, bf16[2,576,256]{2,1,0:T(8,128)(2,1)S(1)}, u32[]{:S(2)}, u32[]{:S(2)}) collective-permute-start(bf16[2,576,256]{2,1,0:T(8,128)(2,1)S(1)} %pad_maximum_fusion.14), channel_id=1, source_target_pairs={{0,16},{16,0},{32,48},{48,32},{64,80},{80,64},{96,112},{112,96},{1... | collective-permute-start | bytes 1769480 | tf_op jit(solution)/shard_map/cond/branch_1_fun/ppermute | solution.py:50
  89.9 0.0 collective-permute-done.22.refs_8_
  90.0 1.2 pad_maximum_fusion.8
  91.2 4.1 %collective-permute-start.23 = (bf16[4,576,256]{2,1,0:T(8,128)(2,1)}, bf16[4,576,256]{2,1,0:T(8,128)(2,1)}, u32[]{:S(2)}, u32[]{:S(2)}) collective-permute-start(bf16[4,576,256]{2,1,0:T(8,128)(2,1)} %pad_maximum_fusion.8), channel_id=1, source_target_pairs={{0,48},{16,32},{32,16},{48,0},{64,112},{80,96},{96,80},{112,64},{1... | collective-permute-start | bytes 3538952 | tf_op jit(solution)/shard_map/cond/branch_1_fun/ppermute | solution.py:50
  95.3 2.6 %collective-permute-done.24.refs_10_ = bf16[2,576,256]{2,1,0:T(8,128)(2,1)S(1)} collective-permute-done((bf16[2,576,256]{2,1,0:T(8,128)(2,1)S(1)}, bf16[2,576,256]{2,1,0:T(8,128)(2,1)S(1)}, u32[]{:S(2)}, u32[]{:S(2)}) %collective-permute-start.24) | collective-permute-done | bytes 589856 | tf_op jit(solution)/shard_map/cond/branch_1_fun/ppermute | solution.py:50
  97.9 1.2 pad_maximum_fusion.9
  99.1 2.5 %collective-permute-start.25 = (bf16[4,576,256]{2,1,0:T(8,128)(2,1)}, bf16[4,576,256]{2,1,0:T(8,128)(2,1)}, u32[]{:S(2)}, u32[]{:S(2)}) collective-permute-start(bf16[4,576,256]{2,1,0:T(8,128)(2,1)} %pad_maximum_fusion.9), channel_id=1, source_target_pairs={{0,16},{16,0},{32,48},{48,32},{64,80},{80,64},{96,112},{112,96},{1... | collective-permute-start | bytes 3538952 | tf_op jit(solution)/shard_map/cond/branch_1_fun/ppermute | solution.py:50
  101.6 8.9 %collective-permute-done.28.refs_14_ = bf16[2,576,256]{2,1,0:T(8,128)(2,1)S(1)} collective-permute-done((bf16[2,576,256]{2,1,0:T(8,128)(2,1)S(1)}, bf16[2,576,256]{2,1,0:T(8,128)(2,1)S(1)}, u32[]{:S(2)}, u32[]{:S(2)}) %collective-permute-start.28) | collective-permute-done | bytes 589856 | tf_op jit(solution)/shard_map/cond/branch_1_fun/ppermute | solution.py:50
  110.5 1.2 pad_maximum_fusion.11
  111.8 2.7 %collective-permute-start.29 = (bf16[4,576,256]{2,1,0:T(8,128)(2,1)}, bf16[4,576,256]{2,1,0:T(8,128)(2,1)}, u32[]{:S(2)}, u32[]{:S(2)}) collective-permute-start(bf16[4,576,256]{2,1,0:T(8,128)(2,1)} %pad_maximum_fusion.11), channel_id=1, source_target_pairs={{0,16},{16,0},{32,48},{48,32},{64,80},{80,64},{96,112},{112,96},{1... | collective-permute-start | bytes 3538952 | tf_op jit(solution)/shard_map/cond/branch_1_fun/ppermute | solution.py:50
  114.4 0.0 collective-permute-done.26.refs_12_
  114.5 1.2 pad_maximum_fusion.10
  115.7 4.6 %collective-permute-start.27 = (bf16[4,576,256]{2,1,0:T(8,128)(2,1)}, bf16[4,576,256]{2,1,0:T(8,128)(2,1)}, u32[]{:S(2)}, u32[]{:S(2)}) collective-permute-start(bf16[4,576,256]{2,1,0:T(8,128)(2,1)} %pad_maximum_fusion.10), channel_id=1, source_target_pairs={{0,48},{16,32},{32,16},{48,0},{64,112},{80,96},{96,80},{112,64},{1... | collective-permute-start | bytes 3538952 | tf_op jit(solution)/shard_map/cond/branch_1_fun/ppermute | solution.py:50
  120.3 0.6 fusion.5.slot_ref
  120.8 15.1 %collective-permute-done.23.refs_9_ = bf16[4,576,256]{2,1,0:T(8,128)(2,1)} collective-permute-done((bf16[4,576,256]{2,1,0:T(8,128)(2,1)}, bf16[4,576,256]{2,1,0:T(8,128)(2,1)}, u32[]{:S(2)}, u32[]{:S(2)}) %collective-permute-start.23) | collective-permute-done | bytes 1179680 | tf_op jit(solution)/shard_map/cond/branch_1_fun/ppermute | solution.py:50
  135.9 0.0 collective-permute-done.25.refs_11_
  135.9 17.2 %collective-permute-done.29.refs_15_ = bf16[4,576,256]{2,1,0:T(8,128)(2,1)} collective-permute-done((bf16[4,576,256]{2,1,0:T(8,128)(2,1)}, bf16[4,576,256]{2,1,0:T(8,128)(2,1)}, u32[]{:S(2)}, u32[]{:S(2)}) %collective-permute-start.29) | collective-permute-done | bytes 1179680 | tf_op jit(solution)/shard_map/cond/branch_1_fun/ppermute | solution.py:50
  153.1 7.2 %collective-permute-done.27.refs_13_ = bf16[4,576,256]{2,1,0:T(8,128)(2,1)} collective-permute-done((bf16[4,576,256]{2,1,0:T(8,128)(2,1)}, bf16[4,576,256]{2,1,0:T(8,128)(2,1)}, u32[]{:S(2)}, u32[]{:S(2)}) %collective-permute-start.27) | collective-permute-done | bytes 1179680 | tf_op jit(solution)/shard_map/cond/branch_1_fun/ppermute | solution.py:50
  160.3 20.2 %weight_grads.5 = bf16[2,4,2,2,32,8,128]{6,5,4,3,2,1,0:T(8,128)(2,1)} custom-call(s32[32]{0:T(128)} %fusion.5.slot_ref, s32[1]{0:T(128)} %bitcast.9.core_ref, bf16[576,256]{1,0:T(8,128)(2,1)} %copy-done.50, bf16[576,256]{1,0:T(8,128)(2,1)} %copy-done.22, bf16[576,256]{1,0:T(8,128)(2,1)} %copy-done.24, bf16[576,256]{1,0:T(8,128)(2,1)} %copy-done.26, ...), custom_call_target="tpu_custom_call" | custom-call | tf_op jit(solution)/shard_map/cond/branch_1_fun/weight_grads/pallas_call | solution.py:189
  180.7 1.4 slice_bitcast_fusion.3
  182.1 1.9 collective-permute-start.60
  184.1 2.6 %collective-permute-done.60 = bf16[4,2,2,32,8,128]{5,4,3,2,1,0:T(8,128)(2,1)S(1)} collective-permute-done((bf16[4,2,2,32,8,128]{5,4,3,2,1,0:T(8,128)(2,1)S(1)}, bf16[4,2,2,32,8,128]{5,4,3,2,1,0:T(8,128)(2,1)S(1)}, u32[]{:S(2)}, u32[]{:S(2)}) %collective-permute-start.60) | collective-permute-done | bytes 1048608 | tf_op jit(solution)/shard_map/ppermute | solution.py:243
  186.7 1.3 fusion.12
  188.0 3.5 %all-to-all-start.1 = ((bf16[4,2,2,32,8,128]{5,4,3,2,1,0:T(8,128)(2,1)}), bf16[4,2,2,32,8,128]{5,4,3,2,1,0:T(8,128)(2,1)S(1)}, u32[]{:S(2)}, u32[]{:S(2)}) async-start(bf16[4,2,2,32,8,128]{5,4,3,2,1,0:T(8,128)(2,1)} %fusion.12), calls=%async_computation.1 | async-start | bytes 2097152 | tf_op jit(solution)/shard_map/all_to_all | solution.py:246
  191.5 15.6 %all-to-all-done.1 = bf16[4,2,2,32,8,128]{5,4,3,2,1,0:T(8,128)(2,1)S(1)} async-done(((bf16[4,2,2,32,8,128]{5,4,3,2,1,0:T(8,128)(2,1)}), bf16[4,2,2,32,8,128]{5,4,3,2,1,0:T(8,128)(2,1)S(1)}, u32[]{:S(2)}, u32[]{:S(2)}) %all-to-all-start.1) | async-done | bytes 1048608 | tf_op jit(solution)/shard_map/all_to_all | solution.py:246
  207.1 0.2 convert_reduce_fusion
  207.3 1.9 collective-permute-start.61
  209.3 19.7 %collective-permute-done.61 = bf16[2,32,8,128]{3,2,1,0:T(8,128)(2,1)S(1)} collective-permute-done((bf16[2,32,8,128]{3,2,1,0:T(8,128)(2,1)S(1)}, bf16[2,32,8,128]{3,2,1,0:T(8,128)(2,1)S(1)}, u32[]{:S(2)}, u32[]{:S(2)}) %collective-permute-start.61) | collective-permute-done | bytes 131104 | tf_op jit(solution)/shard_map/ppermute | solution.py:251
  229.0 0.7 slice_bitcast_fusion.5
  (39 shorter events, 0.2 us)
Async XLA Ops:
  0.6 7.5 %copy-start = (s32[8]{0:T(128)S(1)}, s32[8]{0:T(128)}, u32[]{:S(2)}) copy-start(s32[8]{0:T(128)} %constant.98.clone) | copy-start | bytes 100
  0.6 7.4 %copy-start.57 = (s32[32]{0:T(128)S(1)}, s32[32]{0:T(128)}, u32[]{:S(2)}) copy-start(s32[32]{0:T(128)} %param.15) | copy-start | bytes 388
  1.3 21.2 %copy-start.1 = (bf16[32,128,128]{2,1,0:T(8,128)(2,1)S(1)}, bf16[32,128,128]{2,1,0:T(8,128)(2,1)}, u32[]{:S(2)}) copy-start(bf16[32,128,128]{2,1,0:T(8,128)(2,1)} %param.13) | copy-start | bytes 3145732
  1.3 21.2 %copy-start.2 = (bf16[32,128,128]{2,1,0:T(8,128)(2,1)S(1)}, bf16[32,128,128]{2,1,0:T(8,128)(2,1)}, u32[]{:S(2)}) copy-start(bf16[32,128,128]{2,1,0:T(8,128)(2,1)} %param.14) | copy-start | bytes 3145732
  3.8 13.6 %all-to-all-start = ((bf16[8,104,256]{2,1,0:T(8,128)(2,1)}), bf16[8,104,256]{2,1,0:T(8,128)(2,1)S(1)}, u32[]{:S(2)}, u32[]{:S(2)}) async-start(bf16[8,104,256]{2,1,0:T(8,128)(2,1)} %bitcast.119), calls=%async_computation | async-start | bytes 851968 | tf_op jit(solution)/shard_map/all_to_all | solution.py:217
  17.4 0.8 copy-start.48
  22.6 61.2 %copy-start.50 = (bf16[576,256]{1,0:T(8,128)(2,1)}, bf16[576,256]{1,0:T(8,128)(2,1)S(1)}, u32[]{:S(2)}) copy-start(bf16[576,256]{1,0:T(8,128)(2,1)S(1)} %get-tuple-element.298.refs_0_) | copy-start | bytes 884740 | tf_op jit(solution)/shard_map/cond
  22.6 19.4 %collective-permute-start.15 = (bf16[576,256]{1,0:T(8,128)(2,1)S(1)}, bf16[576,256]{1,0:T(8,128)(2,1)S(1)}, u32[]{:S(2)}, u32[]{:S(2)}) collective-permute-start(bf16[576,256]{1,0:T(8,128)(2,1)S(1)} %get-tuple-element.298.refs_0_), channel_id=1, source_target_pairs={{0,128},{16,144},{32,160},{48,176},{64,0},{80,16},{96,32},{112,48}... | collective-permute-start | bytes 884744 | tf_op jit(solution)/shard_map/cond/branch_1_fun/ppermute | solution.py:45
  27.8 17.8 %collective-permute-start.19 = (bf16[576,256]{1,0:T(8,128)(2,1)S(1)}, bf16[576,256]{1,0:T(8,128)(2,1)S(1)}, u32[]{:S(2)}, u32[]{:S(2)}) collective-permute-start(bf16[576,256]{1,0:T(8,128)(2,1)S(1)} %get-tuple-element.298.refs_0_), channel_id=1, source_target_pairs={{0,64},{16,80},{32,96},{48,112},{64,192},{80,208},{96,224},{112,24... | collective-permute-start | bytes 884744 | tf_op jit(solution)/shard_map/cond/branch_1_fun/ppermute | solution.py:45
  42.0 47.9 %copy-start.22 = (bf16[576,256]{1,0:T(8,128)(2,1)}, bf16[576,256]{1,0:T(8,128)(2,1)S(1)}, u32[]{:S(2)}) copy-start(bf16[576,256]{1,0:T(8,128)(2,1)S(1)} %collective-permute-done.15.refs_1_) | copy-start | bytes 884740 | tf_op jit(solution)/shard_map/cond
  42.0 17.8 %collective-permute-start.16 = (bf16[576,256]{1,0:T(8,128)(2,1)S(1)}, bf16[576,256]{1,0:T(8,128)(2,1)S(1)}, u32[]{:S(2)}, u32[]{:S(2)}) collective-permute-start(bf16[576,256]{1,0:T(8,128)(2,1)S(1)} %collective-permute-done.15.refs_1_), channel_id=1, source_target_pairs={{0,128},{16,144},{32,160},{48,176},{64,0},{80,16},{96,32},{112,48}... | collective-permute-start | bytes 884744 | tf_op jit(solution)/shard_map/cond/branch_1_fun/ppermute | solution.py:45
  45.6 52.3 %copy-start.23 = (bf16[576,256]{1,0:T(8,128)(2,1)}, bf16[576,256]{1,0:T(8,128)(2,1)S(1)}, u32[]{:S(2)}) copy-start(bf16[576,256]{1,0:T(8,128)(2,1)S(1)} %collective-permute-done.19.refs_7_) | copy-start | bytes 884740 | tf_op jit(solution)/shard_map/cond
  45.6 18.2 %collective-permute-start.20 = (bf16[576,256]{1,0:T(8,128)(2,1)S(1)}, bf16[576,256]{1,0:T(8,128)(2,1)S(1)}, u32[]{:S(2)}, u32[]{:S(2)}) collective-permute-start(bf16[576,256]{1,0:T(8,128)(2,1)S(1)} %collective-permute-done.19.refs_7_), channel_id=1, source_target_pairs={{0,64},{16,80},{32,96},{48,112},{64,192},{80,208},{96,224},{112,24... | collective-permute-start | bytes 884744 | tf_op jit(solution)/shard_map/cond/branch_1_fun/ppermute | solution.py:45
  59.9 38.0 %copy-start.24 = (bf16[576,256]{1,0:T(8,128)(2,1)}, bf16[576,256]{1,0:T(8,128)(2,1)S(1)}, u32[]{:S(2)}) copy-start(bf16[576,256]{1,0:T(8,128)(2,1)S(1)} %collective-permute-done.16.refs_2_) | copy-start | bytes 884740 | tf_op jit(solution)/shard_map/cond
  59.9 15.4 %collective-permute-start.17 = (bf16[576,256]{1,0:T(8,128)(2,1)S(1)}, bf16[576,256]{1,0:T(8,128)(2,1)S(1)}, u32[]{:S(2)}, u32[]{:S(2)}) collective-permute-start(bf16[576,256]{1,0:T(8,128)(2,1)S(1)} %collective-permute-done.16.refs_2_), channel_id=1, source_target_pairs={{0,128},{16,144},{32,160},{48,176},{64,0},{80,16},{96,32},{112,48}... | collective-permute-start | bytes 884744 | tf_op jit(solution)/shard_map/cond/branch_1_fun/ppermute | solution.py:45
  63.8 46.7 %copy-start.25 = (bf16[576,256]{1,0:T(8,128)(2,1)}, bf16[576,256]{1,0:T(8,128)(2,1)S(1)}, u32[]{:S(2)}) copy-start(bf16[576,256]{1,0:T(8,128)(2,1)S(1)} %collective-permute-done.20.refs_6_) | copy-start | bytes 884740 | tf_op jit(solution)/shard_map/cond
  63.8 19.9 %collective-permute-start.21 = (bf16[576,256]{1,0:T(8,128)(2,1)S(1)}, bf16[576,256]{1,0:T(8,128)(2,1)S(1)}, u32[]{:S(2)}, u32[]{:S(2)}) collective-permute-start(bf16[576,256]{1,0:T(8,128)(2,1)S(1)} %collective-permute-done.20.refs_6_), channel_id=1, source_target_pairs={{0,64},{16,80},{32,96},{48,112},{64,192},{80,208},{96,224},{112,24... | collective-permute-start | bytes 884744 | tf_op jit(solution)/shard_map/cond/branch_1_fun/ppermute | solution.py:45
  67.9 22.0 %collective-permute-start.22 = (bf16[2,576,256]{2,1,0:T(8,128)(2,1)S(1)}, bf16[2,576,256]{2,1,0:T(8,128)(2,1)S(1)}, u32[]{:S(2)}, u32[]{:S(2)}) collective-permute-start(bf16[2,576,256]{2,1,0:T(8,128)(2,1)S(1)} %pad_maximum_fusion.12), channel_id=1, source_target_pairs={{0,16},{16,0},{32,48},{48,32},{64,80},{80,64},{96,112},{112,96},{1... | collective-permute-start | bytes 1769480 | tf_op jit(solution)/shard_map/cond/branch_1_fun/ppermute | solution.py:50
  75.3 39.2 %copy-start.26 = (bf16[576,256]{1,0:T(8,128)(2,1)}, bf16[576,256]{1,0:T(8,128)(2,1)S(1)}, u32[]{:S(2)}) copy-start(bf16[576,256]{1,0:T(8,128)(2,1)S(1)} %collective-permute-done.17.refs_3_) | copy-start | bytes 884740 | tf_op jit(solution)/shard_map/cond
  75.3 10.7 %collective-permute-start.18 = (bf16[576,256]{1,0:T(8,128)(2,1)S(1)}, bf16[576,256]{1,0:T(8,128)(2,1)S(1)}, u32[]{:S(2)}, u32[]{:S(2)}) collective-permute-start(bf16[576,256]{1,0:T(8,128)(2,1)S(1)} %collective-permute-done.17.refs_3_), channel_id=1, source_target_pairs={{0,128},{16,144},{32,160},{48,176},{64,0},{80,16},{96,32},{112,48}... | collective-permute-start | bytes 884744 | tf_op jit(solution)/shard_map/cond/branch_1_fun/ppermute | solution.py:45
  77.2 20.7 %collective-permute-start.24 = (bf16[2,576,256]{2,1,0:T(8,128)(2,1)S(1)}, bf16[2,576,256]{2,1,0:T(8,128)(2,1)S(1)}, u32[]{:S(2)}, u32[]{:S(2)}) collective-permute-start(bf16[2,576,256]{2,1,0:T(8,128)(2,1)S(1)} %pad_maximum_fusion.13), channel_id=1, source_target_pairs={{0,48},{16,32},{32,16},{48,0},{64,112},{80,96},{96,80},{112,64},{1... | collective-permute-start | bytes 1769480 | tf_op jit(solution)/shard_map/cond/branch_1_fun/ppermute | solution.py:50
  83.8 26.8 %copy-start.27 = (bf16[576,256]{1,0:T(8,128)(2,1)}, bf16[576,256]{1,0:T(8,128)(2,1)S(1)}, u32[]{:S(2)}) copy-start(bf16[576,256]{1,0:T(8,128)(2,1)S(1)} %collective-permute-done.21.refs_5_) | copy-start | bytes 884740 | tf_op jit(solution)/shard_map/cond
  83.8 26.7 %collective-permute-start.28 = (bf16[2,576,256]{2,1,0:T(8,128)(2,1)S(1)}, bf16[2,576,256]{2,1,0:T(8,128)(2,1)S(1)}, u32[]{:S(2)}, u32[]{:S(2)}) collective-permute-start(bf16[2,576,256]{2,1,0:T(8,128)(2,1)S(1)} %pad_maximum_fusion.15), channel_id=1, source_target_pairs={{0,48},{16,32},{32,16},{48,0},{64,112},{80,96},{96,80},{112,64},{1... | collective-permute-start | bytes 1769480 | tf_op jit(solution)/shard_map/cond/branch_1_fun/ppermute | solution.py:50
  86.0 28.5 %copy-start.28 = (bf16[576,256]{1,0:T(8,128)(2,1)}, bf16[576,256]{1,0:T(8,128)(2,1)S(1)}, u32[]{:S(2)}) copy-start(bf16[576,256]{1,0:T(8,128)(2,1)S(1)} %collective-permute-done.18.refs_4_) | copy-start | bytes 884740 | tf_op jit(solution)/shard_map/cond
  86.0 28.4 %collective-permute-start.26 = (bf16[2,576,256]{2,1,0:T(8,128)(2,1)S(1)}, bf16[2,576,256]{2,1,0:T(8,128)(2,1)S(1)}, u32[]{:S(2)}, u32[]{:S(2)}) collective-permute-start(bf16[2,576,256]{2,1,0:T(8,128)(2,1)S(1)} %pad_maximum_fusion.14), channel_id=1, source_target_pairs={{0,16},{16,0},{32,48},{48,32},{64,80},{80,64},{96,112},{112,96},{1... | collective-permute-start | bytes 1769480 | tf_op jit(solution)/shard_map/cond/branch_1_fun/ppermute | solution.py:50
  90.0 9.2 %copy-start.40 = (bf16[2,576,256]{2,1,0:T(8,128)(2,1)}, bf16[2,576,256]{2,1,0:T(8,128)(2,1)S(1)}, u32[]{:S(2)}) copy-start(bf16[2,576,256]{2,1,0:T(8,128)(2,1)S(1)} %collective-permute-done.22.refs_8_) | copy-start | bytes 1769476 | tf_op jit(solution)/shard_map/cond
  91.2 44.7 %collective-permute-start.23 = (bf16[4,576,256]{2,1,0:T(8,128)(2,1)}, bf16[4,576,256]{2,1,0:T(8,128)(2,1)}, u32[]{:S(2)}, u32[]{:S(2)}) collective-permute-start(bf16[4,576,256]{2,1,0:T(8,128)(2,1)} %pad_maximum_fusion.8), channel_id=1, source_target_pairs={{0,48},{16,32},{32,16},{48,0},{64,112},{80,96},{96,80},{112,64},{1... | collective-permute-start | bytes 3538952 | tf_op jit(solution)/shard_map/cond/branch_1_fun/ppermute | solution.py:50
  97.9 13.9 %copy-start.41 = (bf16[2,576,256]{2,1,0:T(8,128)(2,1)}, bf16[2,576,256]{2,1,0:T(8,128)(2,1)S(1)}, u32[]{:S(2)}) copy-start(bf16[2,576,256]{2,1,0:T(8,128)(2,1)S(1)} %collective-permute-done.24.refs_10_) | copy-start | bytes 1769476 | tf_op jit(solution)/shard_map/cond
  99.1 36.8 %collective-permute-start.25 = (bf16[4,576,256]{2,1,0:T(8,128)(2,1)}, bf16[4,576,256]{2,1,0:T(8,128)(2,1)}, u32[]{:S(2)}, u32[]{:S(2)}) collective-permute-start(bf16[4,576,256]{2,1,0:T(8,128)(2,1)} %pad_maximum_fusion.9), channel_id=1, source_target_pairs={{0,16},{16,0},{32,48},{48,32},{64,80},{80,64},{96,112},{112,96},{1... | collective-permute-start | bytes 3538952 | tf_op jit(solution)/shard_map/cond/branch_1_fun/ppermute | solution.py:50
  110.5 5.2 %copy-start.42 = (bf16[2,576,256]{2,1,0:T(8,128)(2,1)}, bf16[2,576,256]{2,1,0:T(8,128)(2,1)S(1)}, u32[]{:S(2)}) copy-start(bf16[2,576,256]{2,1,0:T(8,128)(2,1)S(1)} %collective-permute-done.28.refs_14_) | copy-start | bytes 1769476 | tf_op jit(solution)/shard_map/cond
  111.8 8.5 %copy-start.54 = (s32[32]{0:T(128)S(1)}, s32[32]{0:T(128)}, u32[]{:S(2)}) copy-start(s32[32]{0:T(128)} %get-tuple-element.186) | copy-start | bytes 388 | tf_op jit(solution)/shard_map/cond
  111.8 41.3 %collective-permute-start.29 = (bf16[4,576,256]{2,1,0:T(8,128)(2,1)}, bf16[4,576,256]{2,1,0:T(8,128)(2,1)}, u32[]{:S(2)}, u32[]{:S(2)}) collective-permute-start(bf16[4,576,256]{2,1,0:T(8,128)(2,1)} %pad_maximum_fusion.11), channel_id=1, source_target_pairs={{0,16},{16,0},{32,48},{48,32},{64,80},{80,64},{96,112},{112,96},{1... | collective-permute-start | bytes 3538952 | tf_op jit(solution)/shard_map/cond/branch_1_fun/ppermute | solution.py:50
  114.5 5.8 %copy-start.43 = (bf16[2,576,256]{2,1,0:T(8,128)(2,1)}, bf16[2,576,256]{2,1,0:T(8,128)(2,1)S(1)}, u32[]{:S(2)}) copy-start(bf16[2,576,256]{2,1,0:T(8,128)(2,1)S(1)} %collective-permute-done.26.refs_12_) | copy-start | bytes 1769476 | tf_op jit(solution)/shard_map/cond
  115.7 44.6 %collective-permute-start.27 = (bf16[4,576,256]{2,1,0:T(8,128)(2,1)}, bf16[4,576,256]{2,1,0:T(8,128)(2,1)}, u32[]{:S(2)}, u32[]{:S(2)}) collective-permute-start(bf16[4,576,256]{2,1,0:T(8,128)(2,1)} %pad_maximum_fusion.10), channel_id=1, source_target_pairs={{0,48},{16,32},{32,16},{48,0},{64,112},{80,96},{96,80},{112,64},{1... | collective-permute-start | bytes 3538952 | tf_op jit(solution)/shard_map/cond/branch_1_fun/ppermute | solution.py:50
  180.7 6.0 %copy-start.3 = (bf16[2,4,2,2,32,8,128]{6,5,4,3,2,1,0:T(8,128)(2,1)S(1)}, bf16[2,4,2,2,32,8,128]{6,5,4,3,2,1,0:T(8,128)(2,1)}, u32[]{:S(2)}) copy-start(bf16[2,4,2,2,32,8,128]{6,5,4,3,2,1,0:T(8,128)(2,1)} %get-tuple-element.307) | copy-start | bytes 6291460
  182.1 4.6 %collective-permute-start.60 = (bf16[4,2,2,32,8,128]{5,4,3,2,1,0:T(8,128)(2,1)S(1)}, bf16[4,2,2,32,8,128]{5,4,3,2,1,0:T(8,128)(2,1)S(1)}, u32[]{:S(2)}, u32[]{:S(2)}) collective-permute-start(bf16[4,2,2,32,8,128]{5,4,3,2,1,0:T(8,128)(2,1)S(1)} %slice_bitcast_fusion.3), channel_id=1, source_target_pairs={{0,1},{1,0},{2,3},{3,2},{4,5},{5,4},{6,7},{7,6},{8,9},{9,8},{10,11... | collective-permute-start | bytes 3145736 | tf_op jit(solution)/shard_map/ppermute | solution.py:243
  188.0 19.2 %all-to-all-start.1 = ((bf16[4,2,2,32,8,128]{5,4,3,2,1,0:T(8,128)(2,1)}), bf16[4,2,2,32,8,128]{5,4,3,2,1,0:T(8,128)(2,1)S(1)}, u32[]{:S(2)}, u32[]{:S(2)}) async-start(bf16[4,2,2,32,8,128]{5,4,3,2,1,0:T(8,128)(2,1)} %fusion.12), calls=%async_computation.1 | async-start | bytes 2097152 | tf_op jit(solution)/shard_map/all_to_all | solution.py:246
  207.3 21.6 %collective-permute-start.61 = (bf16[2,32,8,128]{3,2,1,0:T(8,128)(2,1)S(1)}, bf16[2,32,8,128]{3,2,1,0:T(8,128)(2,1)S(1)}, u32[]{:S(2)}, u32[]{:S(2)}) collective-permute-start(bf16[2,32,8,128]{3,2,1,0:T(8,128)(2,1)S(1)} %fusion.14), channel_id=1, source_target_pairs={{0,8},{1,9},{2,10},{3,11},{4,12},{5,13},{6,14},{7,15},{8,0},{9,1},... | collective-permute-start | bytes 393224 | tf_op jit(solution)/shard_map/ppermute | solution.py:251
where the time goes:
time: 230 us
  waiting for transfers between devices  121 us (53%)
  starting transfers between devices  66.6 us (29%)
  Pallas kernels  25.8 us (11%)
  other arithmetic  8.41 us (4%)
  local copies, waits for them, and re-layouts  4.86 us (2%)
    ppermute x8, waiting for transfers between devices, swap_y(): return lax.ppermute(value, 'blk', pairs)  51 us
    ppermute x8, starting transfers between devices, swap_y(): return lax.ppermute(value, 'blk', pairs)  29.2 us
    ppermute x7, waiting for transfers between devices, move_z(): return lax.ppermute(value, 'blk', pairs)  25.8 us
    ppermute x7, starting transfers between devices, move_z(): return lax.ppermute(value, 'blk', pairs)  25.7 us
    pallas_call x1, Pallas kernels, gather_and_differentiate(): pl.pallas_call(grad_kernel, out_shape=jax.ShapeDtypeStruct((2, N_X, 2, 2,...  20.2 us
    ppermute x1, waiting for transfers between devices, shards(): theirs = lax.ppermute(theirs.astype(jnp.bfloat16), 'seq', across)  19.7 us
    all_to_all x1, waiting for transfers between devices, shards(): lax.all_to_all(total, 'seq', 0, 0, axis_index_groups=along_x, tiled=True)  15.6 us
    all_to_all x1, waiting for transfers between devices, shards(): lax.all_to_all(dealt, 'seq', 0, 0, axis_index_groups=halves, tiled=True)  6.63 us
  transfers between devices with their start and end apart: 19, of which 13 were waited for; matrix products, arithmetic and copies ran while one was open for 4% of the time, Pallas kernels for 0%

commit v1 on v0

--- a/solution.py
+++ b/solution.py
@@ -17,7 +17,6 @@
 LIVE = 7680
 SIZES = (512, 576, 640, 768)
 NOTE_ROWS = 8
-CHUNKS = 4
 DEAD = 256.0
 RING = (0, 2, 4, 6, 7, 5, 3, 1)
 PLACE = tuple(RING.index(z) for z in range(N_Z))
@@ -103,77 +102,102 @@
     ).astype(jnp.bfloat16)
 
 
-def grad_kernel(slot_ref, core_ref, *refs):
-    rows_at_once = refs[0].shape[0] // CHUNKS
-    own = refs[:N_Z]
-    passed = refs[N_Z : N_Z + 2 * len(BATCHES)]
-    w_in_ref, w_out_ref, out_ref, held, hidden, summed, sems = refs[N_Z + 2 * len(BATCHES) :]
-    copies = []
-
-    def put(source, target):
-        copies.append(pltpu.make_async_copy(source, target, sems.at[len(copies)]))
-
+def whereabouts():
+    found = [0] * (N_Z * N_Y)
     for slot in range(N_Z):
-        put(own[slot], held.at[slot * N_Y])
+        found[slot * N_Y] = 4 * slot
     for index, (batch, mask) in enumerate(BATCHES):
-        near, far = passed[2 * index : 2 * index + 2]
+        near = 4 * (N_Z + 2 * index)
         for i, slot in enumerate(batch):
-            put(near.at[i], held.at[slot * N_Y + mask])
-            put(far.at[i], held.at[slot * N_Y + (mask ^ 2)])
-            put(far.at[i + len(batch)], held.at[slot * N_Y + 2])
-    for copy in copies:
-        copy.start()
-    for copy in copies:
-        copy.wait()
-    core = core_ref[0]
-
-    @pl.loop(0, w_in_ref.shape[0] // PER_COLUMN)
+            found[slot * N_Y + mask] = near + i
+            found[slot * N_Y + (mask ^ 2)] = near + 4 + i
+            found[slot * N_Y + 2] = near + 4 + len(batch) + i
+    return found
+
+
+def grad_kernel(where_ref, *refs):
+    n_held = N_Z + 2 * len(BATCHES)
+    held = refs[:n_held]
+    w_in_ref, w_out_ref, even, odd, four, sems = refs[n_held:]
+    groups = even.shape[3] // PER_COLUMN
+
+    def fetch(group, into):
+        for r in range(PER_COLUMN):
+            where = where_ref[group * PER_COLUMN + r]
+            for i, ref in enumerate(held):
+
+                def start(ref=ref, r=r, where=where):
+                    block = ref if len(ref.shape) == 2 else ref.at[where % 4]
+                    pltpu.make_async_copy(block, four.at[into, r], sems.at[into, r]).start()
+
+                pl.when(where // 4 == i)(start)
+
+    fetch(0, 0)
+
+    @pl.loop(0, groups)
     def _(group):
+        now = group % 2
+
+        @pl.when(group + 1 < groups)
+        def _():
+            fetch(group + 1, 1 - now)
+
+        for r in range(PER_COLUMN):
+            pltpu.make_async_copy(held[0], four.at[now, r], sems.at[now, r]).wait()
         first = group * PER_COLUMN
-        slots = [slot_ref[first + r] for r in range(PER_COLUMN)]
+        x = jnp.concatenate([four[now, r, :, :SIDE] for r in range(PER_COLUMN)], axis=1)
+        g = jnp.concatenate([four[now, r, :, SIDE:] for r in range(PER_COLUMN)], axis=1)
         w_in = jnp.concatenate([w_in_ref[first + r] for r in range(PER_COLUMN)], axis=0)
         w_out = jnp.concatenate([w_out_ref[first + r] for r in range(PER_COLUMN)], axis=1)
-
-        @pl.loop(0, CHUNKS)
-        def _(chunk):
-            at = pl.ds(pl.multiple_of(chunk * rows_at_once, 16), rows_at_once)
-            x = jnp.concatenate([held[s, at, :SIDE] for s in slots], axis=1)
-            g = jnp.concatenate([held[s, at, SIDE:] for s in slots], axis=1)
-            pre_act = jnp.dot(x, w_in, preferred_element_type=jnp.float32)
-            activation, gelu_slope = gelu_pair(pre_act)
-            grad_act = lax.dot_general(
-                g, w_out, (((1,), (1,)), ((), ())), preferred_element_type=jnp.float32
-            )
-            hidden[0, at] = (grad_act * gelu_slope).astype(jnp.bfloat16)
-            hidden[1, at] = activation.astype(jnp.bfloat16)
-
-        x = jnp.concatenate([held[s, :, :SIDE] for s in slots], axis=1)
-        g = jnp.concatenate([held[s, :, SIDE:] for s in slots], axis=1)
+        pre_act = jnp.dot(x, w_in, preferred_element_type=jnp.float32)
+        activation, gelu_slope = gelu_pair(pre_act)
+        grad_act = lax.dot_general(
+            g, w_out, (((1,), (1,)), ((), ())), preferred_element_type=jnp.float32
+        )
+        grad_pre = (grad_act * gelu_slope).astype(jnp.bfloat16)
         over_rows = (((0,), (0,)), ((), ()))
         shares = (
-            lax.dot_general(hidden[0], x, over_rows, preferred_element_type=jnp.float32),
-            lax.dot_general(hidden[1], g, over_rows, preferred_element_type=jnp.float32),
+            lax.dot_general(grad_pre, x, over_rows, preferred_element_type=jnp.float32),
+            lax.dot_general(
+                activation.astype(jnp.bfloat16), g, over_rows, preferred_element_type=jnp.float32
+            ),
         )
         for which, share in enumerate(shares):
             for r in range(PER_COLUMN):
-                summed[which, r] = share[:, r * SIDE : (r + 1) * SIDE]
-
-        @pl.loop(0, PER_COLUMN)
-        def _(r):
-            for which in range(2):
-                block = summed[which, r]
+                block = share[:, r * SIDE : (r + 1) * SIDE]
                 block = (block.T if which == 0 else block).astype(jnp.bfloat16)
                 for seq in range(N_SEQ):
-                    z_at, x_at, piece = seq // 8, seq % 8 // 2, seq % 2
-                    out_ref[jnp.bitwise_xor(core, piece), x_at, z_at, which, first + r] = block[
+                    target = odd if seq % 2 else even
+                    target[seq % 8 // 2, seq // 8, which, first + r] = block[
                         seq * 8 : seq * 8 + 8
                     ]
 
 
-def gather_and_differentiate(size, packed, slots, core, w_in, w_out):
+def add_cores(even, odd, seq):
+    swap = [(i, i ^ 1) for i in range(N_SEQ)]
+    at_odd = seq % 2 == 1
+    theirs = lax.ppermute(jnp.where(at_odd, even, odd), "seq", swap)
+    mine = jnp.where(at_odd, odd, even)
+    return (mine.astype(jnp.float32) + theirs.astype(jnp.float32)).astype(jnp.bfloat16)
+
+
+def add_along_x(total):
+    along_x = [[h * 8 + x * 2 + c for x in range(N_X)] for h in range(2) for c in range(2)]
+    total = lax.all_to_all(total, "seq", 0, 0, axis_index_groups=along_x, tiled=True)
+    return total.astype(jnp.float32).sum(0)
+
+
+def add_halves(total, seq):
+    across = [(i, i ^ 8) for i in range(N_SEQ)]
+    at_high = seq >= N_DEAL
+    theirs = jnp.where(at_high, total[0], total[1]).astype(jnp.bfloat16)
+    theirs = lax.ppermute(theirs, "seq", across)
+    return (jnp.where(at_high, total[1], total[0]) + theirs.astype(jnp.float32)).astype(jnp.bfloat16)
+
+
+def gather_and_differentiate(size, packed, slots, w_in, w_out):
     vmem = pl.BlockSpec(memory_space=pltpu.VMEM)
     smem = pl.BlockSpec(memory_space=pltpu.SMEM)
-    any_space = pl.BlockSpec(memory_space=pl.ANY)
     n_slots = w_in.shape[0]
     blocks = {0: packed[:size]}
     for i in range(1, 5):
@@ -186,19 +210,19 @@
         near = swap_y(value, mask)
         far = swap_y(jnp.concatenate([value, near]), mask ^ 2)
         passed += [near, far]
+    any_space = pl.BlockSpec(memory_space=pl.ANY)
+    piece = jax.ShapeDtypeStruct((N_X, 2, 2, n_slots, 8, SIDE), jnp.bfloat16)
     return pl.pallas_call(
         grad_kernel,
-        out_shape=jax.ShapeDtypeStruct((2, N_X, 2, 2, n_slots, 8, SIDE), jnp.bfloat16),
-        in_specs=[smem, smem] + [any_space] * (N_Z + len(passed)) + [vmem, vmem],
-        out_specs=vmem,
+        out_shape=[piece] * 2,
+        in_specs=[smem] + [any_space] * (N_Z + len(passed)) + [vmem] * 2,
+        out_specs=[vmem] * 2,
         scratch_shapes=[
-            pltpu.VMEM((N_Y * N_Z, size, 2 * SIDE), jnp.bfloat16),
-            pltpu.VMEM((2, size, SIDE), jnp.bfloat16),
-            pltpu.VMEM((2, PER_COLUMN, SIDE, SIDE), jnp.float32),
-            pltpu.SemaphoreType.DMA((N_Y * N_Z,)),
+            pltpu.VMEM((2, PER_COLUMN, size, 2 * SIDE), jnp.bfloat16),
+            pltpu.SemaphoreType.DMA((2, PER_COLUMN)),
         ],
         name="weight_grads",
-    )(slots, core, *[blocks[i] for i in range(N_Z)], *passed, w_in, w_out)
+    )(slots, *[blocks[i] for i in range(N_Z)], *passed, w_in, w_out)
 
 
 def shards(tokens, grad_out, input_weight_blocks, output_weight_blocks, row_ids, lengths):
@@ -229,27 +253,16 @@
     place = jnp.array(PLACE, jnp.int32)
     z_slot = (place[blk // N_Y] - place[row_ids // N_Y]) % N_Z
     slots = (z_slot * N_Y + jnp.bitwise_xor(blk, row_ids) % N_Y).astype(jnp.int32)
-    shares = lax.switch(
+    slots = jnp.array(whereabouts(), jnp.int32)[slots]
+    even, odd = lax.switch(
         size[0],
         [functools.partial(gather_and_differentiate, n) for n in SIZES],
         packed,
         slots,
-        (seq % 2).reshape(1),
         input_weight_blocks,
         output_weight_blocks,
     )
-
-    swap = [(i, i ^ 1) for i in range(N_SEQ)]
-    other = lax.ppermute(shares[1], "seq", swap)
-    total = (shares[0].astype(jnp.float32) + other.astype(jnp.float32)).astype(jnp.bfloat16)
-    along_x = [[h * 8 + x * 2 + c for x in range(N_X)] for h in range(2) for c in range(2)]
-    total = lax.all_to_all(total, "seq", 0, 0, axis_index_groups=along_x, tiled=True)
-    total = total.astype(jnp.float32).sum(0)
-    mine = lax.dynamic_index_in_dim(total, seq // 8, 0, keepdims=False)
-    theirs = lax.dynamic_index_in_dim(total, 1 - seq // 8, 0, keepdims=False)
-    across = [(i, i ^ 8) for i in range(N_SEQ)]
-    theirs = lax.ppermute(theirs.astype(jnp.bfloat16), "seq", across)
-    total = (mine + theirs.astype(jnp.float32)).astype(jnp.bfloat16)
+    total = add_halves(add_along_x(add_cores(even, odd, seq)), seq)
     return total[0], total[1]
 
 

time: 230 us -> 209 us (0.909)
  waiting for transfers between devices: 121 us -> 110 us
  Pallas kernels: 25.8 us -> 16.2 us
  other arithmetic: 8.41 us -> 4.34 us
  starting transfers between devices: 66.6 us -> 70.5 us
    pallas_call x1, Pallas kernels: 20.2 us -> 10.7 us  [gather_and_differentiate(): pl.pallas_call(grad_kernel, out_shape=[piece] * 2, in_specs=[smem] + [any...]
    ppermute x8, waiting for transfers between devices: 51 us -> 45.2 us  [swap_y(): return lax.ppermute(value, 'blk', pairs)]
    ppermute x7, waiting for transfers between devices: 25.8 us -> 20.7 us  [move_z(): return lax.ppermute(value, 'blk', pairs)]
    concatenate x4, other arithmetic: 4.85 us -> 0.42 us  [gather_and_differentiate(): far = swap_y(jnp.concatenate([value, near]), mask ^ 2)]
  transfers between devices with their start and end apart: 19 -> 19, of which waited for: 13 -> 12; matrix products, arithmetic and copies ran while one was open for 4% -> 2% of each run, Pallas kernels for 0% -> 0%
where the time goes in v1:
time: 209 us; the launch traced here: 208 us
  waiting for transfers between devices  110 us (53%)
  starting transfers between devices  70.5 us (34%)
  Pallas kernels  16.2 us (8%)
  local copies, waits for them, and re-layouts  4.49 us (2%)
  other arithmetic  4.34 us (2%)
  between operations  2.14 us (1%)
    ppermute x8, waiting for transfers between devices, swap_y(): return lax.ppermute(value, 'blk', pairs)  45.2 us
    ppermute x8, starting transfers between devices, swap_y(): return lax.ppermute(value, 'blk', pairs)  31.2 us
    ppermute x7, starting transfers between devices, move_z(): return lax.ppermute(value, 'blk', pairs)  25.7 us
    ppermute x7, waiting for transfers between devices, move_z(): return lax.ppermute(value, 'blk', pairs)  20.7 us
    ppermute x1, waiting for transfers between devices, add_halves(): theirs = lax.ppermute(theirs, 'seq', across)  19.2 us
    all_to_all x1, waiting for transfers between devices, add_along_x(): lax.all_to_all(total, 'seq', 0, 0, axis_index_groups=along_x, tiled=True)  15.6 us
    pallas_call x1, Pallas kernels, gather_and_differentiate(): pl.pallas_call(grad_kernel, out_shape=[piece] * 2, in_specs=[smem] + [any...  10.7 us
    all_to_all x1, waiting for transfers between devices, shards(): lax.all_to_all(dealt, 'seq', 0, 0, axis_index_groups=halves, tiled=True)  6.55 us
  transfers between devices with their start and end apart: 19, of which 12 were waited for; matrix products, arithmetic and copies ran while one was open for 2% of the time, Pallas kernels for 0%

profile of v1, /device:TPU:128, one launch (start us, length us, event | category | flops | bytes accessed | tf_op | source)
XLA Modules:
  0.0 208.1 jit_solution(10388585533275593427)
XLA Ops:
  0.6 0.0 copy-start.1
  0.6 0.0 copy-start
  0.7 0.0 copy-start.69
  1.3 2.3 %deal.1 = bf16[832,256]{1,0:T(8,128)(2,1)} custom-call(s32[1]{0:T(128)S(6)} %copy.18.length_ref, bf16[768,128]{1,0:T(8,128)(2,1)} %tokens_ref.1, bf16[768,128]{1,0:T(8,128)(2,1)} %grad_ref.1), custom_call_target="tpu_custom_call" | custom-call | tf_op jit(solution)/shard_map/deal/pallas_call | solution.py:233
  3.6 4.4 %all-to-all-start = ((bf16[8,104,256]{2,1,0:T(8,128)(2,1)}), bf16[8,104,256]{2,1,0:T(8,128)(2,1)S(1)}, u32[]{:S(2)}, u32[]{:S(2)}) async-start(bf16[8,104,256]{2,1,0:T(8,128)(2,1)} %bitcast.108), calls=%async_computation | async-start | bytes 851968 | tf_op jit(solution)/shard_map/all_to_all | solution.py:241
  8.1 0.0 copy-done.1
  8.1 0.6 dynamic_slice.3
  8.7 0.7 gather_fusion
  9.4 0.7 compare_select_fusion
  10.1 0.7 gather_fusion.1
  10.8 6.5 %all-to-all-done = bf16[8,104,256]{2,1,0:T(8,128)(2,1)S(1)} async-done(((bf16[8,104,256]{2,1,0:T(8,128)(2,1)}), bf16[8,104,256]{2,1,0:T(8,128)(2,1)S(1)}, u32[]{:S(2)}, u32[]{:S(2)}) %all-to-all-start) | async-done | bytes 426016 | tf_op jit(solution)/shard_map/all_to_all | solution.py:241
  17.4 0.8 copy-done.49
  18.1 3.2 %pack.1 = (bf16[768,256]{1,0:T(8,128)(2,1)S(1)}, s32[1]{0:T(128)}) custom-call(bf16[832,256]{1,0:T(8,128)(2,1)} %bitcast.107), custom_call_target="tpu_custom_call" | custom-call | tf_op jit(solution)/shard_map/pack/pallas_call | solution.py:242
  22.0 135.9 %conditional.1 = ((bf16[4,2,2,32,8,128]{5,4,3,2,1,0:T(8,128)(2,1)S(1)}, bf16[4,2,2,32,8,128]{5,4,3,2,1,0:T(8,128)(2,1)})) conditional(s32[]{:T(128)} %bitcast.34, (bf16[768,256]{1,0:T(8,128)(2,1)S(1)}, s32[32]{0:T(128)S(1)}, bf16[32,128,128]{2,1,0:T(8,128)(2,1)S(1)}, bf16[32,128,128]{2,1,0:T(8,128)(2,1)S(1)}) %tuple.38, ...), branch_computations={%region_0.1_spmd, %region_1.2_spmd, %region_2.3_spmd, %region_3.4_... | conditional | flops 7864320 | bytes 116392944 | solution.py:257
  22.1 5.2 %collective-permute-start = (bf16[512,256]{1,0:T(8,128)(2,1)S(1)}, bf16[512,256]{1,0:T(8,128)(2,1)S(1)}, u32[]{:S(2)}, u32[]{:S(2)}) collective-permute-start(bf16[512,256]{1,0:T(8,128)(2,1)S(1)} %get-tuple-element.59.refs_0_), channel_id=1, source_target_pairs={{0,128},{16,144},{32,160},{48,176},{64,0},{80,16},{96,32},{112,48}... | collective-permute-start | bytes 786440 | tf_op jit(solution)/shard_map/cond/branch_0_fun/ppermute | solution.py:44
  27.2 2.8 %collective-permute-start.4 = (bf16[512,256]{1,0:T(8,128)(2,1)S(1)}, bf16[512,256]{1,0:T(8,128)(2,1)S(1)}, u32[]{:S(2)}, u32[]{:S(2)}) collective-permute-start(bf16[512,256]{1,0:T(8,128)(2,1)S(1)} %get-tuple-element.59.refs_0_), channel_id=1, source_target_pairs={{0,64},{16,80},{32,96},{48,112},{64,192},{80,208},{96,224},{112,24... | collective-permute-start | bytes 786440 | tf_op jit(solution)/shard_map/cond/branch_0_fun/ppermute | solution.py:44
  30.0 9.6 %collective-permute-done.refs_1_ = bf16[512,256]{1,0:T(8,128)(2,1)S(1)} collective-permute-done((bf16[512,256]{1,0:T(8,128)(2,1)S(1)}, bf16[512,256]{1,0:T(8,128)(2,1)S(1)}, u32[]{:S(2)}, u32[]{:S(2)}) %collective-permute-start) | collective-permute-done | bytes 262176 | tf_op jit(solution)/shard_map/cond/branch_0_fun/ppermute | solution.py:44
  39.6 4.0 %collective-permute-start.1 = (bf16[512,256]{1,0:T(8,128)(2,1)S(1)}, bf16[512,256]{1,0:T(8,128)(2,1)S(1)}, u32[]{:S(2)}, u32[]{:S(2)}) collective-permute-start(bf16[512,256]{1,0:T(8,128)(2,1)S(1)} %collective-permute-done.refs_1_), channel_id=1, source_target_pairs={{0,128},{16,144},{32,160},{48,176},{64,0},{80,16},{96,32},{112,48}... | collective-permute-start | bytes 786440 | tf_op jit(solution)/shard_map/cond/branch_0_fun/ppermute | solution.py:44
  43.6 0.0 collective-permute-done.4.refs_7_
  43.6 3.9 %collective-permute-start.5 = (bf16[512,256]{1,0:T(8,128)(2,1)S(1)}, bf16[512,256]{1,0:T(8,128)(2,1)S(1)}, u32[]{:S(2)}, u32[]{:S(2)}) collective-permute-start(bf16[512,256]{1,0:T(8,128)(2,1)S(1)} %collective-permute-done.4.refs_7_), channel_id=1, source_target_pairs={{0,64},{16,80},{32,96},{48,112},{64,192},{80,208},{96,224},{112,24... | collective-permute-start | bytes 786440 | tf_op jit(solution)/shard_map/cond/branch_0_fun/ppermute | solution.py:44
  47.6 8.5 %collective-permute-done.1.refs_2_ = bf16[512,256]{1,0:T(8,128)(2,1)S(1)} collective-permute-done((bf16[512,256]{1,0:T(8,128)(2,1)S(1)}, bf16[512,256]{1,0:T(8,128)(2,1)S(1)}, u32[]{:S(2)}, u32[]{:S(2)}) %collective-permute-start.1) | collective-permute-done | bytes 262176 | tf_op jit(solution)/shard_map/cond/branch_0_fun/ppermute | solution.py:44
  56.1 4.1 %collective-permute-start.2 = (bf16[512,256]{1,0:T(8,128)(2,1)S(1)}, bf16[512,256]{1,0:T(8,128)(2,1)S(1)}, u32[]{:S(2)}, u32[]{:S(2)}) collective-permute-start(bf16[512,256]{1,0:T(8,128)(2,1)S(1)} %collective-permute-done.1.refs_2_), channel_id=1, source_target_pairs={{0,128},{16,144},{32,160},{48,176},{64,0},{80,16},{96,32},{112,48}... | collective-permute-start | bytes 786440 | tf_op jit(solution)/shard_map/cond/branch_0_fun/ppermute | solution.py:44
  60.2 0.0 collective-permute-done.5.refs_6_
  60.2 3.9 %collective-permute-start.6 = (bf16[512,256]{1,0:T(8,128)(2,1)S(1)}, bf16[512,256]{1,0:T(8,128)(2,1)S(1)}, u32[]{:S(2)}, u32[]{:S(2)}) collective-permute-start(bf16[512,256]{1,0:T(8,128)(2,1)S(1)} %collective-permute-done.5.refs_6_), channel_id=1, source_target_pairs={{0,64},{16,80},{32,96},{48,112},{64,192},{80,208},{96,224},{112,24... | collective-permute-start | bytes 786440 | tf_op jit(solution)/shard_map/cond/branch_0_fun/ppermute | solution.py:44
  64.1 0.1 pad_maximum_fusion.4
  64.2 3.5 %collective-permute-start.7 = (bf16[2,512,256]{2,1,0:T(8,128)(2,1)S(1)}, bf16[2,512,256]{2,1,0:T(8,128)(2,1)S(1)}, u32[]{:S(2)}, u32[]{:S(2)}) collective-permute-start(bf16[2,512,256]{2,1,0:T(8,128)(2,1)S(1)} %pad_maximum_fusion.4), channel_id=1, source_target_pairs={{0,16},{16,0},{32,48},{48,32},{64,80},{80,64},{96,112},{112,96},{1... | collective-permute-start | bytes 1572872 | tf_op jit(solution)/shard_map/cond/branch_0_fun/ppermute | solution.py:49
  67.7 2.5 %collective-permute-done.2.refs_3_ = bf16[512,256]{1,0:T(8,128)(2,1)S(1)} collective-permute-done((bf16[512,256]{1,0:T(8,128)(2,1)S(1)}, bf16[512,256]{1,0:T(8,128)(2,1)S(1)}, u32[]{:S(2)}, u32[]{:S(2)}) %collective-permute-start.2) | collective-permute-done | bytes 262176 | tf_op jit(solution)/shard_map/cond/branch_0_fun/ppermute | solution.py:44
  70.2 1.9 collective-permute-start.3
  72.1 0.1 pad_maximum_fusion.5
  72.2 7.0 %collective-permute-start.9 = (bf16[2,512,256]{2,1,0:T(8,128)(2,1)S(1)}, bf16[2,512,256]{2,1,0:T(8,128)(2,1)S(1)}, u32[]{:S(2)}, u32[]{:S(2)}) collective-permute-start(bf16[2,512,256]{2,1,0:T(8,128)(2,1)S(1)} %pad_maximum_fusion.5), channel_id=1, source_target_pairs={{0,48},{16,32},{32,16},{48,0},{64,112},{80,96},{96,80},{112,64},{1... | collective-permute-start | bytes 1572872 | tf_op jit(solution)/shard_map/cond/branch_0_fun/ppermute | solution.py:49
  79.2 0.0 collective-permute-done.6.refs_5_
  79.2 0.1 pad_maximum_fusion.7
  79.3 1.9 collective-permute-start.13
  81.2 0.0 collective-permute-done.3.refs_4_
  81.2 0.1 pad_maximum_fusion.6
  81.3 5.2 %collective-permute-start.11 = (bf16[2,512,256]{2,1,0:T(8,128)(2,1)S(1)}, bf16[2,512,256]{2,1,0:T(8,128)(2,1)S(1)}, u32[]{:S(2)}, u32[]{:S(2)}) collective-permute-start(bf16[2,512,256]{2,1,0:T(8,128)(2,1)S(1)} %pad_maximum_fusion.6), channel_id=1, source_target_pairs={{0,16},{16,0},{32,48},{48,32},{64,80},{80,64},{96,112},{112,96},{1... | collective-permute-start | bytes 1572872 | tf_op jit(solution)/shard_map/cond/branch_0_fun/ppermute | solution.py:49
  86.5 0.0 collective-permute-done.7.refs_8_
  86.5 0.1 pad_maximum_fusion
  86.6 4.1 %collective-permute-start.8 = (bf16[4,512,256]{2,1,0:T(8,128)(2,1)S(1)}, bf16[4,512,256]{2,1,0:T(8,128)(2,1)S(1)}, u32[]{:S(2)}, u32[]{:S(2)}) collective-permute-start(bf16[4,512,256]{2,1,0:T(8,128)(2,1)S(1)} %pad_maximum_fusion), channel_id=1, source_target_pairs={{0,48},{16,32},{32,16},{48,0},{64,112},{80,96},{96,80},{112,64},{1... | collective-permute-start | bytes 3145736 | tf_op jit(solution)/shard_map/cond/branch_0_fun/ppermute | solution.py:49
  90.7 1.3 collective-permute-done.9.refs_10_
  92.0 0.1 pad_maximum_fusion.1
  92.1 2.5 %collective-permute-start.10 = (bf16[4,512,256]{2,1,0:T(8,128)(2,1)S(1)}, bf16[4,512,256]{2,1,0:T(8,128)(2,1)S(1)}, u32[]{:S(2)}, u32[]{:S(2)}) collective-permute-start(bf16[4,512,256]{2,1,0:T(8,128)(2,1)S(1)} %pad_maximum_fusion.1), channel_id=1, source_target_pairs={{0,16},{16,0},{32,48},{48,32},{64,80},{80,64},{96,112},{112,96},{1... | collective-permute-start | bytes 3145736 | tf_op jit(solution)/shard_map/cond/branch_0_fun/ppermute | solution.py:49
  94.7 8.6 %collective-permute-done.13.refs_14_ = bf16[2,512,256]{2,1,0:T(8,128)(2,1)S(1)} collective-permute-done((bf16[2,512,256]{2,1,0:T(8,128)(2,1)S(1)}, bf16[2,512,256]{2,1,0:T(8,128)(2,1)S(1)}, u32[]{:S(2)}, u32[]{:S(2)}) %collective-permute-start.13) | collective-permute-done | bytes 524320 | tf_op jit(solution)/shard_map/cond/branch_0_fun/ppermute | solution.py:49
  103.3 0.1 pad_maximum_fusion.3
  103.4 2.5 %collective-permute-start.14 = (bf16[4,512,256]{2,1,0:T(8,128)(2,1)S(1)}, bf16[4,512,256]{2,1,0:T(8,128)(2,1)S(1)}, u32[]{:S(2)}, u32[]{:S(2)}) collective-permute-start(bf16[4,512,256]{2,1,0:T(8,128)(2,1)S(1)} %pad_maximum_fusion.3), channel_id=1, source_target_pairs={{0,16},{16,0},{32,48},{48,32},{64,80},{80,64},{96,112},{112,96},{1... | collective-permute-start | bytes 3145736 | tf_op jit(solution)/shard_map/cond/branch_0_fun/ppermute | solution.py:49
  105.9 0.0 collective-permute-done.11.refs_12_
  105.9 0.1 pad_maximum_fusion.2
  106.1 4.6 %collective-permute-start.12 = (bf16[4,512,256]{2,1,0:T(8,128)(2,1)S(1)}, bf16[4,512,256]{2,1,0:T(8,128)(2,1)S(1)}, u32[]{:S(2)}, u32[]{:S(2)}) collective-permute-start(bf16[4,512,256]{2,1,0:T(8,128)(2,1)S(1)} %pad_maximum_fusion.2), channel_id=1, source_target_pairs={{0,48},{16,32},{32,16},{48,0},{64,112},{80,96},{96,80},{112,64},{1... | collective-permute-start | bytes 3145736 | tf_op jit(solution)/shard_map/cond/branch_0_fun/ppermute | solution.py:49
  110.6 15.1 %collective-permute-done.8.refs_9_ = bf16[4,512,256]{2,1,0:T(8,128)(2,1)S(1)} collective-permute-done((bf16[4,512,256]{2,1,0:T(8,128)(2,1)S(1)}, bf16[4,512,256]{2,1,0:T(8,128)(2,1)S(1)}, u32[]{:S(2)}, u32[]{:S(2)}) %collective-permute-start.8) | collective-permute-done | bytes 1048608 | tf_op jit(solution)/shard_map/cond/branch_0_fun/ppermute | solution.py:49
  125.7 0.0 collective-permute-done.10.refs_11_
  125.7 15.3 %collective-permute-done.14.refs_15_ = bf16[4,512,256]{2,1,0:T(8,128)(2,1)S(1)} collective-permute-done((bf16[4,512,256]{2,1,0:T(8,128)(2,1)S(1)}, bf16[4,512,256]{2,1,0:T(8,128)(2,1)S(1)}, u32[]{:S(2)}, u32[]{:S(2)}) %collective-permute-start.14) | collective-permute-done | bytes 1048608 | tf_op jit(solution)/shard_map/cond/branch_0_fun/ppermute | solution.py:49
  141.0 4.9 %collective-permute-done.12.refs_13_ = bf16[4,512,256]{2,1,0:T(8,128)(2,1)S(1)} collective-permute-done((bf16[4,512,256]{2,1,0:T(8,128)(2,1)S(1)}, bf16[4,512,256]{2,1,0:T(8,128)(2,1)S(1)}, u32[]{:S(2)}, u32[]{:S(2)}) %collective-permute-start.12) | collective-permute-done | bytes 1048608 | tf_op jit(solution)/shard_map/cond/branch_0_fun/ppermute | solution.py:49
  145.9 1.0 copy-done.67
  146.9 10.7 %weight_grads.4 = (bf16[4,2,2,32,8,128]{5,4,3,2,1,0:T(8,128)(2,1)S(1)}, bf16[4,2,2,32,8,128]{5,4,3,2,1,0:T(8,128)(2,1)}) custom-call(s32[32]{0:T(128)S(1)} %get-tuple-element.32.where_ref, bf16[512,256]{1,0:T(8,128)(2,1)} %copy-done.68, bf16[512,256]{1,0:T(8,128)(2,1)} %copy-done.38, bf16[512,256]{1,0:T(8,128)(2,1)} %copy-done.40, ...), custom_call_target="tpu_custom_call" | custom-call | tf_op jit(solution)/shard_map/cond/branch_0_fun/weight_grads/pallas_call | solution.py:215
  157.9 1.4 broadcast_select_fusion
  159.3 1.9 collective-permute-start.60
  161.2 2.6 %collective-permute-done.60 = bf16[4,2,2,32,8,128]{5,4,3,2,1,0:T(8,128)(2,1)S(1)} collective-permute-done((bf16[4,2,2,32,8,128]{5,4,3,2,1,0:T(8,128)(2,1)S(1)}, bf16[4,2,2,32,8,128]{5,4,3,2,1,0:T(8,128)(2,1)S(1)}, u32[]{:S(2)}, u32[]{:S(2)}) %collective-permute-start.60) | collective-permute-done | bytes 1048608 | tf_op jit(solution)/shard_map/ppermute | solution.py:179
  163.8 1.4 add_convert_fusion
  165.2 3.5 %all-to-all-start.1 = ((bf16[4,2,2,32,8,128]{5,4,3,2,1,0:T(8,128)(2,1)}), bf16[4,2,2,32,8,128]{5,4,3,2,1,0:T(8,128)(2,1)S(1)}, u32[]{:S(2)}, u32[]{:S(2)}) async-start(bf16[4,2,2,32,8,128]{5,4,3,2,1,0:T(8,128)(2,1)} %add_convert_fusion), calls=%async_computation.1 | async-start | bytes 2097152 | tf_op jit(solution)/shard_map/all_to_all | solution.py:186
  168.8 15.6 %all-to-all-done.1 = bf16[4,2,2,32,8,128]{5,4,3,2,1,0:T(8,128)(2,1)S(1)} async-done(((bf16[4,2,2,32,8,128]{5,4,3,2,1,0:T(8,128)(2,1)}), bf16[4,2,2,32,8,128]{5,4,3,2,1,0:T(8,128)(2,1)S(1)}, u32[]{:S(2)}, u32[]{:S(2)}) %all-to-all-start.1) | async-done | bytes 1048608 | tf_op jit(solution)/shard_map/all_to_all | solution.py:186
  184.4 0.2 convert_reduce_fusion
  184.6 3.6 %collective-permute-start.61 = (bf16[2,32,8,128]{3,2,1,0:T(8,128)(2,1)S(1)}, bf16[2,32,8,128]{3,2,1,0:T(8,128)(2,1)S(1)}, u32[]{:S(2)}, u32[]{:S(2)}) collective-permute-start(bf16[2,32,8,128]{3,2,1,0:T(8,128)(2,1)S(1)} %fusion.1), channel_id=1, source_target_pairs={{0,8},{1,9},{2,10},{3,11},{4,12},{5,13},{6,14},{7,15},{8,0},{9,1},... | collective-permute-start | bytes 393224 | tf_op jit(solution)/shard_map/ppermute | solution.py:194
  188.2 19.2 %collective-permute-done.61 = bf16[2,32,8,128]{3,2,1,0:T(8,128)(2,1)S(1)} collective-permute-done((bf16[2,32,8,128]{3,2,1,0:T(8,128)(2,1)S(1)}, bf16[2,32,8,128]{3,2,1,0:T(8,128)(2,1)S(1)}, u32[]{:S(2)}, u32[]{:S(2)}) %collective-permute-start.61) | collective-permute-done | bytes 131104 | tf_op jit(solution)/shard_map/ppermute | solution.py:194
  207.4 0.7 slice_bitcast_fusion.3
  (46 shorter events, 0.2 us)
Async XLA Ops:
  0.6 7.5 %copy-start.1 = (s32[8]{0:T(128)S(1)}, s32[8]{0:T(128)}, u32[]{:S(2)}) copy-start(s32[8]{0:T(128)} %constant.85.clone) | copy-start | bytes 100
  0.6 9.5 %copy-start = (s32[32]{0:T(128)S(1)}, s32[32]{0:T(128)}, u32[]{:S(2)}) copy-start(s32[32]{0:T(128)} %constant.86.clone) | copy-start | bytes 388
  0.7 7.4 %copy-start.69 = (s32[32]{0:T(128)S(1)}, s32[32]{0:T(128)}, u32[]{:S(2)}) copy-start(s32[32]{0:T(128)} %param.16) | copy-start | bytes 388
  3.6 18.3 %copy-start.2 = (bf16[32,128,128]{2,1,0:T(8,128)(2,1)S(1)}, bf16[32,128,128]{2,1,0:T(8,128)(2,1)}, u32[]{:S(2)}) copy-start(bf16[32,128,128]{2,1,0:T(8,128)(2,1)} %param.14) | copy-start | bytes 3145732
  3.6 18.3 %copy-start.3 = (bf16[32,128,128]{2,1,0:T(8,128)(2,1)S(1)}, bf16[32,128,128]{2,1,0:T(8,128)(2,1)}, u32[]{:S(2)}) copy-start(bf16[32,128,128]{2,1,0:T(8,128)(2,1)} %param.15) | copy-start | bytes 3145732
  3.6 13.7 %all-to-all-start = ((bf16[8,104,256]{2,1,0:T(8,128)(2,1)}), bf16[8,104,256]{2,1,0:T(8,128)(2,1)S(1)}, u32[]{:S(2)}, u32[]{:S(2)}) async-start(bf16[8,104,256]{2,1,0:T(8,128)(2,1)} %bitcast.108), calls=%async_computation | async-start | bytes 851968 | tf_op jit(solution)/shard_map/all_to_all | solution.py:241
  17.4 0.8 copy-start.49
  22.0 25.5 %copy-start.68 = (bf16[512,256]{1,0:T(8,128)(2,1)}, bf16[512,256]{1,0:T(8,128)(2,1)S(1)}, u32[]{:S(2)}) copy-start(bf16[512,256]{1,0:T(8,128)(2,1)S(1)} %get-tuple-element.59.refs_0_) | copy-start | bytes 786436 | tf_op jit(solution)/shard_map/cond
  22.1 17.5 %collective-permute-start = (bf16[512,256]{1,0:T(8,128)(2,1)S(1)}, bf16[512,256]{1,0:T(8,128)(2,1)S(1)}, u32[]{:S(2)}, u32[]{:S(2)}) collective-permute-start(bf16[512,256]{1,0:T(8,128)(2,1)S(1)} %get-tuple-element.59.refs_0_), channel_id=1, source_target_pairs={{0,128},{16,144},{32,160},{48,176},{64,0},{80,16},{96,32},{112,48}... | collective-permute-start | bytes 786440 | tf_op jit(solution)/shard_map/cond/branch_0_fun/ppermute | solution.py:44
  27.2 16.4 %collective-permute-start.4 = (bf16[512,256]{1,0:T(8,128)(2,1)S(1)}, bf16[512,256]{1,0:T(8,128)(2,1)S(1)}, u32[]{:S(2)}, u32[]{:S(2)}) collective-permute-start(bf16[512,256]{1,0:T(8,128)(2,1)S(1)} %get-tuple-element.59.refs_0_), channel_id=1, source_target_pairs={{0,64},{16,80},{32,96},{48,112},{64,192},{80,208},{96,224},{112,24... | collective-permute-start | bytes 786440 | tf_op jit(solution)/shard_map/cond/branch_0_fun/ppermute | solution.py:44
  39.6 46.9 %copy-start.38 = (bf16[512,256]{1,0:T(8,128)(2,1)}, bf16[512,256]{1,0:T(8,128)(2,1)S(1)}, u32[]{:S(2)}) copy-start(bf16[512,256]{1,0:T(8,128)(2,1)S(1)} %collective-permute-done.refs_1_) | copy-start | bytes 786436 | tf_op jit(solution)/shard_map/cond
  39.6 16.5 %collective-permute-start.1 = (bf16[512,256]{1,0:T(8,128)(2,1)S(1)}, bf16[512,256]{1,0:T(8,128)(2,1)S(1)}, u32[]{:S(2)}, u32[]{:S(2)}) collective-permute-start(bf16[512,256]{1,0:T(8,128)(2,1)S(1)} %collective-permute-done.refs_1_), channel_id=1, source_target_pairs={{0,128},{16,144},{32,160},{48,176},{64,0},{80,16},{96,32},{112,48}... | collective-permute-start | bytes 786440 | tf_op jit(solution)/shard_map/cond/branch_0_fun/ppermute | solution.py:44
  43.6 48.4 %copy-start.39 = (bf16[512,256]{1,0:T(8,128)(2,1)}, bf16[512,256]{1,0:T(8,128)(2,1)S(1)}, u32[]{:S(2)}) copy-start(bf16[512,256]{1,0:T(8,128)(2,1)S(1)} %collective-permute-done.4.refs_7_) | copy-start | bytes 786436 | tf_op jit(solution)/shard_map/cond
  43.6 16.6 %collective-permute-start.5 = (bf16[512,256]{1,0:T(8,128)(2,1)S(1)}, bf16[512,256]{1,0:T(8,128)(2,1)S(1)}, u32[]{:S(2)}, u32[]{:S(2)}) collective-permute-start(bf16[512,256]{1,0:T(8,128)(2,1)S(1)} %collective-permute-done.4.refs_7_), channel_id=1, source_target_pairs={{0,64},{16,80},{32,96},{48,112},{64,192},{80,208},{96,224},{112,24... | collective-permute-start | bytes 786440 | tf_op jit(solution)/shard_map/cond/branch_0_fun/ppermute | solution.py:44
  56.1 35.9 %copy-start.40 = (bf16[512,256]{1,0:T(8,128)(2,1)}, bf16[512,256]{1,0:T(8,128)(2,1)S(1)}, u32[]{:S(2)}) copy-start(bf16[512,256]{1,0:T(8,128)(2,1)S(1)} %collective-permute-done.1.refs_2_) | copy-start | bytes 786436 | tf_op jit(solution)/shard_map/cond
  56.1 14.1 %collective-permute-start.2 = (bf16[512,256]{1,0:T(8,128)(2,1)S(1)}, bf16[512,256]{1,0:T(8,128)(2,1)S(1)}, u32[]{:S(2)}, u32[]{:S(2)}) collective-permute-start(bf16[512,256]{1,0:T(8,128)(2,1)S(1)} %collective-permute-done.1.refs_2_), channel_id=1, source_target_pairs={{0,128},{16,144},{32,160},{48,176},{64,0},{80,16},{96,32},{112,48}... | collective-permute-start | bytes 786440 | tf_op jit(solution)/shard_map/cond/branch_0_fun/ppermute | solution.py:44
  60.2 43.0 %copy-start.41 = (bf16[512,256]{1,0:T(8,128)(2,1)}, bf16[512,256]{1,0:T(8,128)(2,1)S(1)}, u32[]{:S(2)}) copy-start(bf16[512,256]{1,0:T(8,128)(2,1)S(1)} %collective-permute-done.5.refs_6_) | copy-start | bytes 786436 | tf_op jit(solution)/shard_map/cond
  60.2 19.0 %collective-permute-start.6 = (bf16[512,256]{1,0:T(8,128)(2,1)S(1)}, bf16[512,256]{1,0:T(8,128)(2,1)S(1)}, u32[]{:S(2)}, u32[]{:S(2)}) collective-permute-start(bf16[512,256]{1,0:T(8,128)(2,1)S(1)} %collective-permute-done.5.refs_6_), channel_id=1, source_target_pairs={{0,64},{16,80},{32,96},{48,112},{64,192},{80,208},{96,224},{112,24... | collective-permute-start | bytes 786440 | tf_op jit(solution)/shard_map/cond/branch_0_fun/ppermute | solution.py:44
  64.2 22.3 %collective-permute-start.7 = (bf16[2,512,256]{2,1,0:T(8,128)(2,1)S(1)}, bf16[2,512,256]{2,1,0:T(8,128)(2,1)S(1)}, u32[]{:S(2)}, u32[]{:S(2)}) collective-permute-start(bf16[2,512,256]{2,1,0:T(8,128)(2,1)S(1)} %pad_maximum_fusion.4), channel_id=1, source_target_pairs={{0,16},{16,0},{32,48},{48,32},{64,80},{80,64},{96,112},{112,96},{1... | collective-permute-start | bytes 1572872 | tf_op jit(solution)/shard_map/cond/branch_0_fun/ppermute | solution.py:49
  70.2 35.7 %copy-start.42 = (bf16[512,256]{1,0:T(8,128)(2,1)}, bf16[512,256]{1,0:T(8,128)(2,1)S(1)}, u32[]{:S(2)}) copy-start(bf16[512,256]{1,0:T(8,128)(2,1)S(1)} %collective-permute-done.2.refs_3_) | copy-start | bytes 786436 | tf_op jit(solution)/shard_map/cond
  70.2 11.0 %collective-permute-start.3 = (bf16[512,256]{1,0:T(8,128)(2,1)S(1)}, bf16[512,256]{1,0:T(8,128)(2,1)S(1)}, u32[]{:S(2)}, u32[]{:S(2)}) collective-permute-start(bf16[512,256]{1,0:T(8,128)(2,1)S(1)} %collective-permute-done.2.refs_3_), channel_id=1, source_target_pairs={{0,128},{16,144},{32,160},{48,176},{64,0},{80,16},{96,32},{112,48}... | collective-permute-start | bytes 786440 | tf_op jit(solution)/shard_map/cond/branch_0_fun/ppermute | solution.py:44
  72.2 19.8 %collective-permute-start.9 = (bf16[2,512,256]{2,1,0:T(8,128)(2,1)S(1)}, bf16[2,512,256]{2,1,0:T(8,128)(2,1)S(1)}, u32[]{:S(2)}, u32[]{:S(2)}) collective-permute-start(bf16[2,512,256]{2,1,0:T(8,128)(2,1)S(1)} %pad_maximum_fusion.5), channel_id=1, source_target_pairs={{0,48},{16,32},{32,16},{48,0},{64,112},{80,96},{96,80},{112,64},{1... | collective-permute-start | bytes 1572872 | tf_op jit(solution)/shard_map/cond/branch_0_fun/ppermute | solution.py:49
  79.2 24.1 %copy-start.43 = (bf16[512,256]{1,0:T(8,128)(2,1)}, bf16[512,256]{1,0:T(8,128)(2,1)S(1)}, u32[]{:S(2)}) copy-start(bf16[512,256]{1,0:T(8,128)(2,1)S(1)} %collective-permute-done.6.refs_5_) | copy-start | bytes 786436 | tf_op jit(solution)/shard_map/cond
  79.3 24.0 %collective-permute-start.13 = (bf16[2,512,256]{2,1,0:T(8,128)(2,1)S(1)}, bf16[2,512,256]{2,1,0:T(8,128)(2,1)S(1)}, u32[]{:S(2)}, u32[]{:S(2)}) collective-permute-start(bf16[2,512,256]{2,1,0:T(8,128)(2,1)S(1)} %pad_maximum_fusion.7), channel_id=1, source_target_pairs={{0,48},{16,32},{32,16},{48,0},{64,112},{80,96},{96,80},{112,64},{1... | collective-permute-start | bytes 1572872 | tf_op jit(solution)/shard_map/cond/branch_0_fun/ppermute | solution.py:49
  81.2 24.7 %copy-start.44 = (bf16[512,256]{1,0:T(8,128)(2,1)}, bf16[512,256]{1,0:T(8,128)(2,1)S(1)}, u32[]{:S(2)}) copy-start(bf16[512,256]{1,0:T(8,128)(2,1)S(1)} %collective-permute-done.3.refs_4_) | copy-start | bytes 786436 | tf_op jit(solution)/shard_map/cond
  81.3 24.6 %collective-permute-start.11 = (bf16[2,512,256]{2,1,0:T(8,128)(2,1)S(1)}, bf16[2,512,256]{2,1,0:T(8,128)(2,1)S(1)}, u32[]{:S(2)}, u32[]{:S(2)}) collective-permute-start(bf16[2,512,256]{2,1,0:T(8,128)(2,1)S(1)} %pad_maximum_fusion.6), channel_id=1, source_target_pairs={{0,16},{16,0},{32,48},{48,32},{64,80},{80,64},{96,112},{112,96},{1... | collective-permute-start | bytes 1572872 | tf_op jit(solution)/shard_map/cond/branch_0_fun/ppermute | solution.py:49
  86.5 5.6 %copy-start.45 = (bf16[2,512,256]{2,1,0:T(8,128)(2,1)}, bf16[2,512,256]{2,1,0:T(8,128)(2,1)S(1)}, u32[]{:S(2)}) copy-start(bf16[2,512,256]{2,1,0:T(8,128)(2,1)S(1)} %collective-permute-done.7.refs_8_) | copy-start | bytes 1572868 | tf_op jit(solution)/shard_map/cond
  86.6 39.1 %collective-permute-start.8 = (bf16[4,512,256]{2,1,0:T(8,128)(2,1)S(1)}, bf16[4,512,256]{2,1,0:T(8,128)(2,1)S(1)}, u32[]{:S(2)}, u32[]{:S(2)}) collective-permute-start(bf16[4,512,256]{2,1,0:T(8,128)(2,1)S(1)} %pad_maximum_fusion), channel_id=1, source_target_pairs={{0,48},{16,32},{32,16},{48,0},{64,112},{80,96},{96,80},{112,64},{1... | collective-permute-start | bytes 3145736 | tf_op jit(solution)/shard_map/cond/branch_0_fun/ppermute | solution.py:49
  92.0 11.3 %copy-start.46 = (bf16[2,512,256]{2,1,0:T(8,128)(2,1)}, bf16[2,512,256]{2,1,0:T(8,128)(2,1)S(1)}, u32[]{:S(2)}) copy-start(bf16[2,512,256]{2,1,0:T(8,128)(2,1)S(1)} %collective-permute-done.9.refs_10_) | copy-start | bytes 1572868 | tf_op jit(solution)/shard_map/cond
  92.1 33.6 %collective-permute-start.10 = (bf16[4,512,256]{2,1,0:T(8,128)(2,1)S(1)}, bf16[4,512,256]{2,1,0:T(8,128)(2,1)S(1)}, u32[]{:S(2)}, u32[]{:S(2)}) collective-permute-start(bf16[4,512,256]{2,1,0:T(8,128)(2,1)S(1)} %pad_maximum_fusion.1), channel_id=1, source_target_pairs={{0,16},{16,0},{32,48},{48,32},{64,80},{80,64},{96,112},{112,96},{1... | collective-permute-start | bytes 3145736 | tf_op jit(solution)/shard_map/cond/branch_0_fun/ppermute | solution.py:49
  103.3 2.8 %copy-start.47 = (bf16[2,512,256]{2,1,0:T(8,128)(2,1)}, bf16[2,512,256]{2,1,0:T(8,128)(2,1)S(1)}, u32[]{:S(2)}) copy-start(bf16[2,512,256]{2,1,0:T(8,128)(2,1)S(1)} %collective-permute-done.13.refs_14_) | copy-start | bytes 1572868 | tf_op jit(solution)/shard_map/cond
  103.4 37.6 %collective-permute-start.14 = (bf16[4,512,256]{2,1,0:T(8,128)(2,1)S(1)}, bf16[4,512,256]{2,1,0:T(8,128)(2,1)S(1)}, u32[]{:S(2)}, u32[]{:S(2)}) collective-permute-start(bf16[4,512,256]{2,1,0:T(8,128)(2,1)S(1)} %pad_maximum_fusion.3), channel_id=1, source_target_pairs={{0,16},{16,0},{32,48},{48,32},{64,80},{80,64},{96,112},{112,96},{1... | collective-permute-start | bytes 3145736 | tf_op jit(solution)/shard_map/cond/branch_0_fun/ppermute | solution.py:49
  105.9 40.0 %copy-start.48 = (bf16[2,512,256]{2,1,0:T(8,128)(2,1)}, bf16[2,512,256]{2,1,0:T(8,128)(2,1)S(1)}, u32[]{:S(2)}) copy-start(bf16[2,512,256]{2,1,0:T(8,128)(2,1)S(1)} %collective-permute-done.11.refs_12_) | copy-start | bytes 1572868 | tf_op jit(solution)/shard_map/cond
  106.1 39.8 %collective-permute-start.12 = (bf16[4,512,256]{2,1,0:T(8,128)(2,1)S(1)}, bf16[4,512,256]{2,1,0:T(8,128)(2,1)S(1)}, u32[]{:S(2)}, u32[]{:S(2)}) collective-permute-start(bf16[4,512,256]{2,1,0:T(8,128)(2,1)S(1)} %pad_maximum_fusion.2), channel_id=1, source_target_pairs={{0,48},{16,32},{32,16},{48,0},{64,112},{80,96},{96,80},{112,64},{1... | collective-permute-start | bytes 3145736 | tf_op jit(solution)/shard_map/cond/branch_0_fun/ppermute | solution.py:49
  125.7 20.2 %copy-start.64 = (bf16[4,512,256]{2,1,0:T(8,128)(2,1)}, bf16[4,512,256]{2,1,0:T(8,128)(2,1)S(1)}, u32[]{:S(2)}) copy-start(bf16[4,512,256]{2,1,0:T(8,128)(2,1)S(1)} %collective-permute-done.8.refs_9_) | copy-start | bytes 3145732 | tf_op jit(solution)/shard_map/cond
  125.7 20.2 %copy-start.65 = (bf16[4,512,256]{2,1,0:T(8,128)(2,1)}, bf16[4,512,256]{2,1,0:T(8,128)(2,1)S(1)}, u32[]{:S(2)}) copy-start(bf16[4,512,256]{2,1,0:T(8,128)(2,1)S(1)} %collective-permute-done.10.refs_11_) | copy-start | bytes 3145732 | tf_op jit(solution)/shard_map/cond
  141.0 4.9 %copy-start.66 = (bf16[4,512,256]{2,1,0:T(8,128)(2,1)}, bf16[4,512,256]{2,1,0:T(8,128)(2,1)S(1)}, u32[]{:S(2)}) copy-start(bf16[4,512,256]{2,1,0:T(8,128)(2,1)S(1)} %collective-permute-done.14.refs_15_) | copy-start | bytes 3145732 | tf_op jit(solution)/shard_map/cond
  145.9 1.0 copy-start.67
  157.8 6.0 %copy-start.4 = (bf16[4,2,2,32,8,128]{5,4,3,2,1,0:T(8,128)(2,1)S(1)}, bf16[4,2,2,32,8,128]{5,4,3,2,1,0:T(8,128)(2,1)}, u32[]{:S(2)}) copy-start(bf16[4,2,2,32,8,128]{5,4,3,2,1,0:T(8,128)(2,1)} %get-tuple-element.56) | copy-start | bytes 3145732
  159.3 4.6 %collective-permute-start.60 = (bf16[4,2,2,32,8,128]{5,4,3,2,1,0:T(8,128)(2,1)S(1)}, bf16[4,2,2,32,8,128]{5,4,3,2,1,0:T(8,128)(2,1)S(1)}, u32[]{:S(2)}, u32[]{:S(2)}) collective-permute-start(bf16[4,2,2,32,8,128]{5,4,3,2,1,0:T(8,128)(2,1)S(1)} %broadcast_select_fusion), channel_id=1, source_target_pairs={{0,1},{1,0},{2,3},{3,2},{4,5},{5,4},{6,7},{7,6},{8,9},{9,8},{10,11... | collective-permute-start | bytes 3145736 | tf_op jit(solution)/shard_map/ppermute | solution.py:179
  165.2 19.2 %all-to-all-start.1 = ((bf16[4,2,2,32,8,128]{5,4,3,2,1,0:T(8,128)(2,1)}), bf16[4,2,2,32,8,128]{5,4,3,2,1,0:T(8,128)(2,1)S(1)}, u32[]{:S(2)}, u32[]{:S(2)}) async-start(bf16[4,2,2,32,8,128]{5,4,3,2,1,0:T(8,128)(2,1)} %add_convert_fusion), calls=%async_computation.1 | async-start | bytes 2097152 | tf_op jit(solution)/shard_map/all_to_all | solution.py:186
  184.6 22.8 %collective-permute-start.61 = (bf16[2,32,8,128]{3,2,1,0:T(8,128)(2,1)S(1)}, bf16[2,32,8,128]{3,2,1,0:T(8,128)(2,1)S(1)}, u32[]{:S(2)}, u32[]{:S(2)}) collective-permute-start(bf16[2,32,8,128]{3,2,1,0:T(8,128)(2,1)S(1)} %fusion.1), channel_id=1, source_target_pairs={{0,8},{1,9},{2,10},{3,11},{4,12},{5,13},{6,14},{7,15},{8,0},{9,1},... | collective-permute-start | bytes 393224 | tf_op jit(solution)/shard_map/ppermute | solution.py:194
